TPU v7x, 256 devices: a whole 4x4x8 slice. The times are simulated.
256 devices in a mesh: bucket: 2 (over core), fsdp: 8 (over z), sp: 16 (over x, y).
Axes of the slice: x: 4, y: 4, z: 8, core: 2. Of those that a mesh axis runs over, the one named last changes fastest.
Arguments:
- hidden_states: bfloat16 [2, 8, 2048, 4096], P('bucket', 'fsdp', 'sp'), may hold values from -60 to 60
- norm_gain: float32 [4096], replicated, may hold values from 0.1 to 1.9
- w_query: bfloat16 [4096, 2048], P(('bucket', 'fsdp'), 'sp'), may hold values from -1 to 1
- w_key: bfloat16 [4096, 512], P(('bucket', 'fsdp'), 'sp'), may hold values from -2 to 2
- w_value: bfloat16 [4096, 512], P(('bucket', 'fsdp'), 'sp'), may hold values from -0.09375 to 0.09375
- out_grad: bfloat16 [2, 8, 2048, 2048], P('bucket', 'fsdp', None, 'sp'), may hold values from -6 to 6
- short_docs: int32 [8, 2048], P('fsdp'), may hold values from 0 to 127, never falling along the last dimension, each value on 1 to 128 neighbouring positions
Outputs:
- attended: bfloat16 [2, 8, 2048, 2048], P('bucket', 'fsdp', None, 'sp')
- grad_query: float32 [4096, 2048], P(('bucket', 'fsdp'), 'sp')
- grad_key: float32 [4096, 512], P(('bucket', 'fsdp'), 'sp')
- grad_value: float32 [4096, 512], P(('bucket', 'fsdp'), 'sp')
All inputs are finite; a program needn't handle non-finite values.
Results may differ from a plain program's by a relative error of at most 0.029.
The roundings to bfloat16 on the way count: a program that leaves them out, or rounds other values in their place, can miss the bound.
Values may be sent and summed in bfloat16 or wider, within the bound.
A program may use at most 128 MiB of HBM per device.

v0:
```python
import math
import functools
import numpy as np
import jax
import jax.numpy as jnp
from jax import lax
from jax.experimental import pallas as pl
from jax.experimental.pallas import tpu as pltpu
from jax.sharding import PartitionSpec as P

DH = 128
SEQ = 2048
QB = 256
KB = 256
NEG = -1e30
SCALE = 1.0 / math.sqrt(DH)
EXP_C = SCALE * math.log2(math.e)


def rope_tables():
    freq = np.float32(500000.0) ** (-2.0 * np.arange(64, dtype=np.float32) / DH)
    freq = np.repeat(freq.astype(np.float64), 2)[None, :]
    sign = np.where(np.arange(DH) % 2 == 0, -1.0, 1.0)[None, :]
    fine = np.arange(128)[:, None] * freq
    coarse = 128 * np.arange(16)[:, None] * freq
    f = np.stack([np.cos(fine), np.sin(fine) * sign]).astype(np.float32)
    c = np.stack([np.cos(coarse), np.sin(coarse) * sign]).astype(np.float32)
    return f, c


def rope_block(fine_ref, coarse_ref, block):
    cf, sf = fine_ref[0], fine_ref[1]
    cc = coarse_ref[0, pl.ds(block, 1), :]
    sc = coarse_ref[1, pl.ds(block, 1), :]
    return cf * cc - sf * sc, sf * cc + cf * sc


def swap_pairs(x):
    lane = lax.broadcasted_iota(jnp.int32, x.shape, 1)
    return jnp.where(lane % 2 == 0, pltpu.roll(x, DH - 1, 1), pltpu.roll(x, 1, 1))


def nn(a, b):
    return jnp.dot(a, b, preferred_element_type=jnp.float32)


def nt(a, b):
    return lax.dot_general(a, b, (((1,), (1,)), ((), ())), preferred_element_type=jnp.float32)


def attention_kernel(q_ref, k_ref, v_ref, g_ref, docs_row, docs_col, fine_ref, coarse_ref,
                     att_ref, dq_ref, dk_ref, dv_ref,
                     kt, vt, s_scr, p_scr, acc, dk_acc, dv_acc):
    bucket = lax.axis_index("bucket")

    @pl.loop(0, SEQ // KB)
    def _(j):
        rows = pl.ds(pl.multiple_of(j * KB, KB), KB)
        kt[j] = k_ref[rows, :].T
        vt[j] = v_ref[rows, :].T

    dk_acc[...] = jnp.zeros_like(dk_acc)
    dv_acc[...] = jnp.zeros_like(dv_acc)

    def finish_query(i, dqt):
        dq = dqt.T * SCALE
        for half in range(QB // 128):
            block = i * (QB // 128) + half
            cos, sin = rope_block(fine_ref, coarse_ref, block)
            x = dq[half * 128:(half + 1) * 128]
            dq_ref[pl.ds(pl.multiple_of(block * 128, 128), 128), :] = (
                x * cos - swap_pairs(x) * sin).astype(jnp.bfloat16)

    @pl.when(bucket == 0)
    def _():
        @pl.loop(0, SEQ // QB)
        def _(i):
            qrows = pl.ds(pl.multiple_of(i * QB, QB), QB)
            q = q_ref[qrows, :]
            g = g_ref[qrows, :]

            def scores(j):
                return nt(k_ref[pl.ds(pl.multiple_of(j * KB, KB), KB), :], q)

            def pass1(j, m):
                s = scores(j)
                s_scr[j] = s
                return jnp.maximum(m, jnp.max(s.reshape(KB // 8, 8, QB), axis=0))

            m8 = lax.fori_loop(0, i, pass1, jnp.full((8, QB), NEG, jnp.float32))
            s = scores(i)
            key = lax.broadcasted_iota(jnp.int32, (KB, QB), 0)
            qry = lax.broadcasted_iota(jnp.int32, (KB, QB), 1)
            s = jnp.where(key <= qry, s, NEG)
            s_scr[i] = s
            m8 = jnp.maximum(m8, jnp.max(s.reshape(KB // 8, 8, QB), axis=0))
            m = jnp.max(m8, axis=0, keepdims=True)
            acc[...] = jnp.zeros_like(acc)

            def pass2(j, l8):
                p = jnp.exp2((s_scr[j] - m) * EXP_C)
                pb = p.astype(jnp.bfloat16)
                p_scr[j] = pb
                acc[...] += nn(vt[j], pb)
                return l8 + jnp.sum(p.reshape(KB // 8, 8, QB), axis=0)

            l8 = lax.fori_loop(0, i + 1, pass2, jnp.zeros((8, QB), jnp.float32))
            rl = 1.0 / jnp.sum(l8, axis=0, keepdims=True)
            ot = acc[...] * rl
            att_ref[qrows, :] = ot.T.astype(jnp.bfloat16)
            gt = (g.astype(jnp.float32).T * rl).astype(jnp.bfloat16)
            gs = gt.T
            d = jnp.sum(ot * gt.astype(jnp.float32), axis=0, keepdims=True)
            acc[...] = jnp.zeros_like(acc)

            @pl.loop(0, i + 1)
            def _(j):
                krows = pl.ds(pl.multiple_of(j * KB, KB), KB)
                pb = p_scr[j]
                dp = nn(v_ref[krows, :], gt)
                ds = (pb.astype(jnp.float32) * (dp - d)).astype(jnp.bfloat16)
                acc[...] += nn(kt[j], ds)
                dk_acc[krows, :] += nn(ds, q)
                dv_acc[krows, :] += nn(pb, gs)

            finish_query(i, acc[...])

    @pl.when(bucket == 1)
    def _():
        span = QB + 128

        @pl.loop(0, SEQ // QB)
        def _(i):
            qrows = pl.ds(pl.multiple_of(i * QB, QB), QB)
            first = pl.multiple_of(jnp.maximum(i * QB - 128, 0), 128)
            krows = pl.ds(first, span)
            q = q_ref[qrows, :]
            g = g_ref[qrows, :]
            k = k_ref[krows, :]
            v = v_ref[krows, :]
            key = lax.broadcasted_iota(jnp.int32, (span, QB), 0) + first
            qry = lax.broadcasted_iota(jnp.int32, (span, QB), 1) + i * QB
            same = docs_col[krows, :] == docs_row[i]
            s = jnp.where((key <= qry) & same, nt(k, q), NEG)
            m = jnp.max(s, axis=0, keepdims=True)
            p = jnp.exp2((s - m) * EXP_C)
            rl = 1.0 / jnp.sum(p, axis=0, keepdims=True)
            pb = p.astype(jnp.bfloat16)
            ot = nn(v.T, pb) * rl
            att_ref[qrows, :] = ot.T.astype(jnp.bfloat16)
            gt = (g.astype(jnp.float32).T * rl).astype(jnp.bfloat16)
            gs = gt.T
            d = jnp.sum(ot * gt.astype(jnp.float32), axis=0, keepdims=True)
            dp = nn(v, gt)
            ds = (pb.astype(jnp.float32) * (dp - d)).astype(jnp.bfloat16)
            finish_query(i, nn(k.T, ds))
            dk_acc[krows, :] += nn(ds, q)
            dv_acc[krows, :] += nn(pb, gs)

    dk_ref[...] = (dk_acc[...] * SCALE).astype(jnp.bfloat16)
    dv_ref[...] = dv_acc[...].astype(jnp.bfloat16)


def attention(q, k, v, g, docs):
    fine, coarse = rope_tables()
    nb = SEQ // KB
    vmem = pl.BlockSpec(memory_space=pltpu.VMEM)
    out = jax.ShapeDtypeStruct((SEQ, DH), jnp.bfloat16)
    return pl.pallas_call(
        attention_kernel,
        out_shape=(out, out, out, out),
        in_specs=[vmem] * 8,
        out_specs=(vmem,) * 4,
        scratch_shapes=[
            pltpu.VMEM((nb, DH, KB), jnp.bfloat16),
            pltpu.VMEM((nb, DH, KB), jnp.bfloat16),
            pltpu.VMEM((nb, KB, QB), jnp.float32),
            pltpu.VMEM((nb, KB, QB), jnp.bfloat16),
            pltpu.VMEM((DH, QB), jnp.float32),
            pltpu.VMEM((SEQ, DH), jnp.float32),
            pltpu.VMEM((SEQ, DH), jnp.float32),
        ],
        compiler_params=pltpu.CompilerParams(vmem_limit_bytes=40 << 20),
        name="attention",
    )(q, k, v, g, docs.reshape(SEQ // QB, 1, QB), docs.reshape(SEQ, 1), jnp.asarray(fine), jnp.asarray(coarse))


HQ = 16
KVH = 4


norm_eps = 1e-05
rope_base = 500000.0


def swapped(value, axis, stride):
    mask = 2**stride
    pairs = [(source, source ^ mask) for source in range(lax.axis_size(axis))]
    return lax.ppermute(value, axis, pairs)


def pair_rotate(values, first_col, sign_factor):
    length, column_total = values.shape
    pair_index = (first_col + 2 * jnp.arange(column_total // 2, dtype=jnp.int32)) % DH // 2
    frequencies = rope_base ** (-2.0 * pair_index.astype(jnp.float32) / DH)
    angles = jnp.arange(length, dtype=jnp.float32)[:, None] * frequencies[None, :]
    cosine = jnp.cos(angles)
    sine_vals = sign_factor * jnp.sin(angles)
    paired = values.reshape(length, column_total // 2, 2)
    even_part = paired[:, :, 0]
    odd_part = paired[:, :, 1]
    turned = jnp.stack(
        [even_part * cosine - odd_part * sine_vals, even_part * sine_vals + odd_part * cosine],
        axis=2,
    )
    return turned.reshape(length, column_total)


def local(hidden_states, norm_gain, w_query, w_key, w_value, out_grad, short_docs):
    tok_rows = hidden_states.shape[2]
    features = hidden_states.shape[3]
    sp_count = lax.axis_size("sp")
    sp_index = lax.axis_index("sp")
    bucket_index = lax.axis_index("bucket")
    local_rows = hidden_states.reshape(tok_rows, features).astype(jnp.float32)
    inv_rms = lax.rsqrt(jnp.mean(local_rows * local_rows, axis=1, keepdims=True) + norm_eps)
    normed_local = (local_rows * inv_rms * norm_gain).astype(jnp.bfloat16)
    normed = lax.all_gather(normed_local, "sp", axis=0, tiled=True)
    seq_len = normed.shape[0]
    q_cols = w_query.shape[1]
    kv_cols = w_key.shape[1]
    pieces = (
        lax.all_gather(w_query, ("bucket", "fsdp"), axis=0, tiled=True),
        lax.all_gather(w_key, ("bucket", "fsdp"), axis=0, tiled=True),
        lax.all_gather(w_value, ("bucket", "fsdp"), axis=0, tiled=True),
    )
    columns = normed
    queries, key_part, value_part = tuple(
        (jnp.dot(columns, piece, preferred_element_type=jnp.float32) for piece in pieces)
    )
    kv_first = sp_index * kv_cols
    query_rot = pair_rotate(queries, 0, 1.0).astype(jnp.bfloat16)
    key_rot = pair_rotate(key_part, kv_first, 1.0).astype(jnp.bfloat16)
    value_own = value_part.astype(jnp.bfloat16)
    heads_dev = q_cols // DH
    group_q = HQ // KVH
    kv_heads_dev = max(1, heads_dev // group_q)
    spread = max(1, sp_count // KVH)
    bit_levels = spread.bit_length() - 1
    key_use = key_rot
    value_use = value_own
    for bit_level in range(bit_levels):
        other_key, other_value = swapped((key_use, value_use), "sp", bit_level)
        upper_half = sp_index // 2**bit_level % 2 == 1
        key_use = jnp.where(
            upper_half,
            jnp.concatenate([other_key, key_use], 1),
            jnp.concatenate([key_use, other_key], 1),
        )
        value_use = jnp.where(
            upper_half,
            jnp.concatenate([other_value, value_use], 1),
            jnp.concatenate([value_use, other_value], 1),
        )
    doc_ids = jnp.where(bucket_index == 0, 0, short_docs[0])
    attended, dquery, dkey_sum, dvalue_sum = attention(query_rot, key_use, value_use, out_grad.reshape(seq_len, q_cols), doc_ids)
    attended = attended.reshape(1, 1, seq_len, q_cols)
    dkey_sum = dkey_sum.astype(jnp.float32)
    dvalue_sum = dvalue_sum.astype(jnp.float32)
    dkey_full = dkey_sum
    dvalue_full = dvalue_sum
    for bit_level in range(bit_levels):
        got_key, got_value = (
            swapped(dkey_full.astype(jnp.bfloat16), "sp", bit_level).astype(dkey_full.dtype),
            swapped(dvalue_full.astype(jnp.bfloat16), "sp", bit_level).astype(dvalue_full.dtype),
        )
        dkey_full = dkey_full + got_key
        dvalue_full = dvalue_full + got_value
    own_start = sp_index % spread * kv_cols
    dkey_cur = lax.dynamic_slice_in_dim(dkey_full, own_start, kv_cols, 1)
    dvalue_cur = lax.dynamic_slice_in_dim(dvalue_full, own_start, kv_cols, 1)
    dkey = pair_rotate(dkey_cur, kv_first, -1.0).astype(jnp.bfloat16)
    dvalue = dvalue_cur.astype(jnp.bfloat16)
    grads_joined = jnp.concatenate([dquery, dkey, dvalue], axis=1)
    columns = normed
    summed = lax.psum_scatter(
        jnp.einsum("tc,tg->cg", columns, grads_joined, preferred_element_type=jnp.float32).astype(
            jnp.bfloat16
        ),
        ("bucket", "fsdp"),
        scatter_dimension=0,
        tiled=True,
    ).astype(jnp.float32)
    return (
        attended,
        summed[:, :q_cols],
        summed[:, q_cols : q_cols + kv_cols],
        summed[:, q_cols + kv_cols :],
    )


def solution(mesh):
    return jax.shard_map(
        local,
        mesh=mesh,
        in_specs=(
            P("bucket", "fsdp", "sp", None),
            P(),
            P(("bucket", "fsdp"), "sp"),
            P(("bucket", "fsdp"), "sp"),
            P(("bucket", "fsdp"), "sp"),
            P("bucket", "fsdp", None, "sp"),
            P("fsdp", None),
        ),
        out_specs=(
            P("bucket", "fsdp", None, "sp"),
            P(("bucket", "fsdp"), "sp"),
            P(("bucket", "fsdp"), "sp"),
            P(("bucket", "fsdp"), "sp"),
        ),
        check_vma=False,
    )
```

profile of v0, /device:TPU:2, one launch (start us, length us, event | category | flops | bytes accessed | tf_op | source)
XLA Modules:
  0.0 389.1 jit_solution(17250042385881983197)
XLA Ops:
  7.2 1.5 fusion
  8.8 2.6 fusion.2
  11.4 0.7 all-gather.5.cloned.1.call-update
  12.3 0.4 copy.53.docs_col
  12.7 30.3 %all_gather.14 = bf16[4096,32]{0,1:T(8,128)(2,1)S(1)} all-gather(bf16[256,32]{0,1:T(8,128)(2,1)S(1)} %copy-done.6), channel_id=1, replica_groups=mesh['bucket'=2,'fsdp'=8,'sp'=16] {'bucket','fsdp'}, dimensions={0}, use_global_device_ids=true | all-gather | bytes 278528 | tf_op jit(solution)/shard_map/all_gather | solution.py:234
  42.9 28.4 %all_gather.15 = bf16[4096,32]{0,1:T(8,128)(2,1)S(1)} all-gather(bf16[256,32]{0,1:T(8,128)(2,1)S(1)} %copy-done.7), channel_id=1, replica_groups=mesh['bucket'=2,'fsdp'=8,'sp'=16] {'bucket','fsdp'}, dimensions={0}, use_global_device_ids=true | all-gather | bytes 278528 | tf_op jit(solution)/shard_map/all_gather | solution.py:235
  71.3 59.3 %all-gather.3.cloned.1.call-done = bf16[2048,4096]{1,0:T(8,128)(2,1)} async-done(((bf16[128,4096]{1,0:T(8,128)(2,1)}), bf16[2048,4096]{1,0:T(8,128)(2,1)}) %all-gather.3.cloned.1.call-update) | async-done | bytes 16777232 | tf_op jit(solution)/shard_map/all_gather | solution.py:228
  130.7 10.8 %fusion.24 = f32[2048,32]{0,1:T(8,128)S(1)} fusion(bf16[2048,4096]{1,0:T(8,128)(2,1)} %all-gather.3.cloned.1.call-done, bf16[4096,32]{0,1:T(8,128)(2,1)S(1)} %all_gather.14), kind=kOutput, calls=%fused_computation.65 | convolution fusion | flops 536870912 | bytes 17301504 | tf_op jit(solution)/shard_map/dot_general | solution.py:239
  141.6 29.2 %all-gather.5.cloned.1.call-done = bf16[4096,128]{1,0:T(8,128)(2,1)} async-done(((bf16[256,128]{1,0:T(8,128)(2,1)}), bf16[4096,128]{1,0:T(8,128)(2,1)}) %all-gather.5.cloned.1.call-update) | async-done | bytes 1048592 | tf_op jit(solution)/shard_map/all_gather | solution.py:233
  170.8 11.7 %fusion.23 = f32[2048,128]{0,1:T(8,128)S(1)} fusion(bf16[2048,4096]{1,0:T(8,128)(2,1)} %all-gather.3.cloned.1.call-done, bf16[4096,128]{1,0:T(8,128)(2,1)} %all-gather.5.cloned.1.call-done), kind=kOutput, calls=%fused_computation.64 | convolution fusion | flops 2147483648 | bytes 18874368 | tf_op jit(solution)/shard_map/dot_general | solution.py:239
  182.5 1.6 reshape.289
  184.1 2.7 fusion.19
  187.0 0.6 subtract_convert_fusion.2
  188.1 1.8 collective-permute-start
  189.8 8.2 %convolution_convert_fusion.1 = bf16[2048,32]{1,0:T(8,128)(2,1)S(1)} fusion(bf16[2048,4096]{1,0:T(8,128)(2,1)} %all-gather.3.cloned.1.call-done, bf16[4096,32]{0,1:T(8,128)(2,1)S(1)} %all_gather.15), kind=kOutput, calls=%fused_computation.3 | convolution fusion | flops 536936448 | bytes 17170432 | tf_op jit(solution)/shard_map/dot_general | solution.py:239
  198.0 0.6 collective-permute-start.2
  198.6 2.4 subtract_convert_fusion
  201.1 2.1 collective-permute-done
  203.1 0.6 maximum_select_fusion
  203.7 3.1 collective-permute-start.1
  206.8 7.6 %collective-permute-done.2 = bf16[2048,32]{1,0:T(8,128)(2,1)S(1)} collective-permute-done((bf16[2048,32]{1,0:T(8,128)(2,1)S(1)}, bf16[2048,32]{1,0:T(8,128)(2,1)S(1)}, u32[]{:S(2)}, u32[]{:S(2)}) %collective-permute-start.2) | collective-permute-done | bytes 131104 | tf_op jit(solution)/shard_map/ppermute | solution.py:199
  214.4 0.6 maximum_select_fusion.2
  215.0 3.1 collective-permute-start.3
  218.2 0.5 copy.44
  218.7 1.0 convert_element_type.83
  219.7 1.3 copy.52.q_ref
  221.0 6.9 %collective-permute-done.1 = bf16[2048,64]{1,0:T(8,128)(2,1)} collective-permute-done((bf16[2048,64]{1,0:T(8,128)(2,1)S(1)}, bf16[2048,64]{1,0:T(8,128)(2,1)}, u32[]{:S(2)}, u32[]{:S(2)}) %collective-permute-start.1) | collective-permute-done | bytes 262176 | tf_op jit(solution)/shard_map/ppermute | solution.py:199
  227.9 1.8 maximum_select_fusion.1.k_ref
  229.7 8.7 %collective-permute-done.3 = bf16[2048,64]{1,0:T(8,128)(2,1)} collective-permute-done((bf16[2048,64]{1,0:T(8,128)(2,1)S(1)}, bf16[2048,64]{1,0:T(8,128)(2,1)}, u32[]{:S(2)}, u32[]{:S(2)}) %collective-permute-start.3) | collective-permute-done | bytes 262176 | tf_op jit(solution)/shard_map/ppermute | solution.py:199
  238.4 1.8 maximum_select_fusion.3.v_ref
  240.2 33.7 %attention.1 = (bf16[2048,128]{1,0:T(8,128)(2,1)}, bf16[2048,128]{1,0:T(8,128)(2,1)S(1)}, bf16[2048,128]{1,0:T(8,128)(2,1)S(1)}, bf16[2048,128]{1,0:T(8,128)(2,1)S(1)}) custom-call(bf16[2048,128]{1,0:T(8,128)(2,1)S(1)} %copy.52.q_ref, bf16[2048,128]{1,0:T(8,128)(2,1)S(1)} %maximum_select_fusion.1.k_ref, bf16[2048,128]{1,0:T(8,128)(2,1)S(1)} %maximum_select_fusion.3.v_ref, ...), custom_call_target="tpu_custom_call" | custom-call | tf_op jit(solution)/shard_map/attention/pallas_call | solution.py:169
  274.2 1.8 collective-permute-start.6
  276.0 7.2 %collective-permute-done.4 = bf16[2048,128]{1,0:T(8,128)(2,1)S(1)} collective-permute-done((bf16[2048,128]{1,0:T(8,128)(2,1)S(1)}, bf16[2048,128]{1,0:T(8,128)(2,1)S(1)}, u32[]{:S(2)}, u32[]{:S(2)}) %collective-permute-start.4) | collective-permute-done | bytes 524320 | tf_op jit(solution)/shard_map/ppermute | solution.py:199
  283.1 1.0 fusion.17
  284.1 0.8 collective-permute-start.5
  284.9 3.8 collective-permute-done.6
  288.8 1.1 fusion.18
  289.9 0.8 collective-permute-start.7
  290.7 4.3 %collective-permute-done.5 = bf16[2048,128]{1,0:T(8,128)(2,1)S(1)} collective-permute-done((bf16[2048,128]{1,0:T(8,128)(2,1)}, bf16[2048,128]{1,0:T(8,128)(2,1)S(1)}, u32[]{:S(2)}, u32[]{:S(2)}) %collective-permute-start.5) | collective-permute-done | bytes 524320 | tf_op jit(solution)/shard_map/ppermute | solution.py:199
  295.0 5.6 %collective-permute-done.7 = bf16[2048,128]{1,0:T(8,128)(2,1)S(1)} collective-permute-done((bf16[2048,128]{1,0:T(8,128)(2,1)S(1)}, bf16[2048,128]{1,0:T(8,128)(2,1)S(1)}, u32[]{:S(2)}, u32[]{:S(2)}) %collective-permute-start.7) | collective-permute-done | bytes 524320 | tf_op jit(solution)/shard_map/ppermute | solution.py:199
  300.6 0.8 copy-done.3
  301.4 3.0 fusion.3
  305.1 0.6 subtract_convert_fusion.1
  306.3 10.5 %convolution_convert_fusion = bf16[4096,192]{0,1:T(8,128)(2,1)} fusion(bf16[2048,4096]{1,0:T(8,128)(2,1)} %all-gather.3.cloned.1.call-done, bf16[2048,32]{1,0:T(8,128)(2,1)S(1)} %copy-done.4, bf16[2048,32]{1,0:T(8,128)(2,1)S(1)} %copy.58, bf16[2048,128]{1,0:T(8,128)(2,1)S(1)} %get-tuple-element.9), kind=kOutput, calls=%fused_computation | convolution fusion | flops 3224371200 | bytes 19136512 | tf_op jit(solution)/shard_map/tc,tg->cg/dot_general | solution.py:287
  316.8 62.8 %reduce-scatter.2.cloned.1.call-done = bf16[256,192]{0,1:T(8,128)(2,1)} async-done(((bf16[4096,192]{0,1:T(8,128)(2,1)}), bf16[256,192]{0,1:T(8,128)(2,1)}) %reduce-scatter.2.cloned.1.call-update) | async-done | bytes 98320 | tf_op jit(solution)/shard_map/reduce_scatter | solution.py:286
  379.6 0.8 slice.42
  380.5 0.8 copy.59
  381.3 1.4 fusion.22
  (40 shorter events, 2.5 us)
Async XLA Ops:
  7.2 5.1 %copy-start.5 = (s32[1,2048]{1,0:T(1,128)S(1)}, s32[1,2048]{1,0:T(1,128)}, u32[]{:S(2)}) copy-start(s32[1,2048]{1,0:T(1,128)} %param.15) | copy-start | bytes 24580
  7.2 5.5 %copy-start.6 = (bf16[256,32]{0,1:T(8,128)(2,1)S(1)}, bf16[256,32]{0,1:T(8,128)(2,1)}, u32[]{:S(2)}) copy-start(bf16[256,32]{0,1:T(8,128)(2,1)} %param.12) | copy-start | bytes 49156
  7.2 35.7 %copy-start.7 = (bf16[256,32]{0,1:T(8,128)(2,1)S(1)}, bf16[256,32]{0,1:T(8,128)(2,1)}, u32[]{:S(2)}) copy-start(bf16[256,32]{0,1:T(8,128)(2,1)} %param.13) | copy-start | bytes 49156
  7.2 123.5 %all-gather.3.cloned.1.call-start = ((), (), s32[]{:S(2)}) async-start(), calls=%async_computation.1 | async-start | bytes 17825792 | tf_op jit(solution)/shard_map/all_gather | solution.py:228
  11.3 159.5 %all-gather.5.cloned.1.call-start = ((), (), s32[]{:S(2)}) async-start(), calls=%async_computation.2 | async-start | bytes 1114112 | tf_op jit(solution)/shard_map/all_gather | solution.py:233
  12.1 367.5 %reduce-scatter.2.cloned.1.call-start = ((), (), s32[]{:S(2)}) async-start(), calls=%async_computation.3 | async-start | bytes 1671168 | tf_op jit(solution)/shard_map/reduce_scatter | solution.py:286
  188.1 15.1 %collective-permute-start = (bf16[2048,32]{1,0:T(8,128)(2,1)S(1)}, bf16[2048,32]{1,0:T(8,128)(2,1)S(1)}, u32[]{:S(2)}, u32[]{:S(2)}) collective-permute-start(bf16[2048,32]{1,0:T(8,128)(2,1)S(1)} %copy.48), channel_id=1, source_target_pairs={{0,1},{1,0},{2,3},{3,2},{4,5},{5,4},{6,7},{7,6},{8,9},{9,8},{10,11... | collective-permute-start | bytes 393224 | tf_op jit(solution)/shard_map/ppermute | solution.py:199
  198.0 16.4 %collective-permute-start.2 = (bf16[2048,32]{1,0:T(8,128)(2,1)S(1)}, bf16[2048,32]{1,0:T(8,128)(2,1)S(1)}, u32[]{:S(2)}, u32[]{:S(2)}) collective-permute-start(bf16[2048,32]{1,0:T(8,128)(2,1)S(1)} %convolution_convert_fusion.1), channel_id=1, source_target_pairs={{0,1},{1,0},{2,3},{3,2},{4,5},{5,4},{6,7},{7,6},{8,9},{9,8},{10,11... | collective-permute-start | bytes 393224 | tf_op jit(solution)/shard_map/ppermute | solution.py:199
  203.7 24.2 %collective-permute-start.1 = (bf16[2048,64]{1,0:T(8,128)(2,1)S(1)}, bf16[2048,64]{1,0:T(8,128)(2,1)}, u32[]{:S(2)}, u32[]{:S(2)}) collective-permute-start(bf16[2048,64]{1,0:T(8,128)(2,1)S(1)} %maximum_select_fusion), channel_id=1, source_target_pairs={{0,2},{1,3},{2,0},{3,1},{4,6},{5,7},{6,4},{7,5},{8,10},{9,11},{10,... | collective-permute-start | bytes 786440 | tf_op jit(solution)/shard_map/ppermute | solution.py:199
  215.0 23.4 %collective-permute-start.3 = (bf16[2048,64]{1,0:T(8,128)(2,1)S(1)}, bf16[2048,64]{1,0:T(8,128)(2,1)}, u32[]{:S(2)}, u32[]{:S(2)}) collective-permute-start(bf16[2048,64]{1,0:T(8,128)(2,1)S(1)} %maximum_select_fusion.2), channel_id=1, source_target_pairs={{0,2},{1,3},{2,0},{3,1},{4,6},{5,7},{6,4},{7,5},{8,10},{9,11},{10,... | collective-permute-start | bytes 786440 | tf_op jit(solution)/shard_map/ppermute | solution.py:199
  218.1 22.1 %copy-start = (bf16[1,1,2048,128]{3,2,1,0:T(8,128)(2,1)S(1)}, bf16[1,1,2048,128]{3,2,1,0:T(8,128)(2,1)}, u32[]{:S(2)}) copy-start(bf16[1,1,2048,128]{3,2,1,0:T(8,128)(2,1)} %param.14) | copy-start | bytes 1572868
  218.1 22.1 %copy-start.1 = (f32[2,128,128]{2,1,0:T(8,128)S(1)}, f32[2,128,128]{2,1,0:T(8,128)}, u32[]{:S(2)}) copy-start(f32[2,128,128]{2,1,0:T(8,128)} %constant.132.clone.fine_ref) | copy-start | bytes 393220
  218.1 22.1 %copy-start.2 = (f32[2,16,128]{2,1,0:T(8,128)S(1)}, f32[2,16,128]{2,1,0:T(8,128)}, u32[]{:S(2)}) copy-start(f32[2,16,128]{2,1,0:T(8,128)} %constant.133.clone.coarse_ref) | copy-start | bytes 49156
  274.0 9.2 %collective-permute-start.4 = (bf16[2048,128]{1,0:T(8,128)(2,1)S(1)}, bf16[2048,128]{1,0:T(8,128)(2,1)S(1)}, u32[]{:S(2)}, u32[]{:S(2)}) collective-permute-start(bf16[2048,128]{1,0:T(8,128)(2,1)S(1)} %get-tuple-element.10), channel_id=1, source_target_pairs={{0,1},{1,0},{2,3},{3,2},{4,5},{5,4},{6,7},{7,6},{8,9},{9,8},{10,11... | collective-permute-start | bytes 1572872 | tf_op jit(solution)/shard_map/ppermute | solution.py:199
  274.2 14.6 %collective-permute-start.6 = (bf16[2048,128]{1,0:T(8,128)(2,1)S(1)}, bf16[2048,128]{1,0:T(8,128)(2,1)S(1)}, u32[]{:S(2)}, u32[]{:S(2)}) collective-permute-start(bf16[2048,128]{1,0:T(8,128)(2,1)S(1)} %get-tuple-element.11), channel_id=1, source_target_pairs={{0,1},{1,0},{2,3},{3,2},{4,5},{5,4},{6,7},{7,6},{8,9},{9,8},{10,11... | collective-permute-start | bytes 1572872 | tf_op jit(solution)/shard_map/ppermute | solution.py:199
  284.1 10.9 %collective-permute-start.5 = (bf16[2048,128]{1,0:T(8,128)(2,1)}, bf16[2048,128]{1,0:T(8,128)(2,1)S(1)}, u32[]{:S(2)}, u32[]{:S(2)}) collective-permute-start(bf16[2048,128]{1,0:T(8,128)(2,1)} %get-tuple-element.30), channel_id=1, source_target_pairs={{0,2},{1,3},{2,0},{3,1},{4,6},{5,7},{6,4},{7,5},{8,10},{9,11},{10,... | collective-permute-start | bytes 1572872 | tf_op jit(solution)/shard_map/ppermute | solution.py:199
  289.9 10.7 %collective-permute-start.7 = (bf16[2048,128]{1,0:T(8,128)(2,1)S(1)}, bf16[2048,128]{1,0:T(8,128)(2,1)S(1)}, u32[]{:S(2)}, u32[]{:S(2)}) collective-permute-start(bf16[2048,128]{1,0:T(8,128)(2,1)S(1)} %get-tuple-element.32), channel_id=1, source_target_pairs={{0,2},{1,3},{2,0},{3,1},{4,6},{5,7},{6,4},{7,5},{8,10},{9,11},{10,... | collective-permute-start | bytes 1572872 | tf_op jit(solution)/shard_map/ppermute | solution.py:199
  300.6 0.8 copy-start.3
  304.5 1.8 copy-start.4
Sparse Core Ops, SparseCore 0:
  11.5 119.1 all-gather.2
  132.5 38.2 all-gather.4
  317.0 62.6 reduce-scatter.1
where the time goes:
time: 390 us; the launch traced here: 389 us
  waiting for transfers between devices  198 us (51%)
  blocking collectives  58.7 us (15%)
  matrix products  41.1 us (11%)
  Pallas kernels  33.7 us (9%)
  other arithmetic  17.7 us (5%)
  between operations  14.1 us (4%)
  local copies, waits for them, and re-layouts  13.3 us (3%)
  starting transfers between devices  12.3 us (3%)
    reduce_scatter x1, waiting for transfers between devices, local(): lax.psum_scatter(jnp.einsum('tc,tg->cg', columns, grads_joined, preferred...  62.8 us
    all_gather x1, waiting for transfers between devices, local(): normed = lax.all_gather(normed_local, 'sp', axis=0, tiled=True)  59.3 us
    ppermute x8, waiting for transfers between devices, swapped(): return lax.ppermute(value, axis, pairs)  46.2 us
    pallas_call x1, Pallas kernels, attention(): pl.pallas_call(attention_kernel, out_shape=(out, out, out, out), in_specs...  33.7 us
    dot_general x3, matrix products, local(): jnp.dot(columns, piece, preferred_element_type=jnp.float32)  30.6 us
    all_gather x1, blocking collectives, local(): lax.all_gather(w_key, ('bucket', 'fsdp'), axis=0, tiled=True)  30.3 us
    all_gather x1, waiting for transfers between devices, local(): lax.all_gather(w_query, ('bucket', 'fsdp'), axis=0, tiled=True)  29.2 us
    all_gather x1, blocking collectives, local(): lax.all_gather(w_value, ('bucket', 'fsdp'), axis=0, tiled=True)  28.4 us
  transfers between devices with their start and end apart: 11, of which 11 were waited for; matrix products, arithmetic and copies ran while one was open for 8% of the time, Pallas kernels for 0%

commit v1 on v0

v1 whole, which is shorter than its diff:
```python
import math
import functools
import numpy as np
import jax
import jax.numpy as jnp
from jax import lax
from jax.experimental import pallas as pl
from jax.experimental.pallas import tpu as pltpu
from jax.sharding import PartitionSpec as P

MESH = pl.DeviceIdType.MESH

DH = 128
SEQ = 2048
QB = 256
KB = 256
NEG = -1e30
SCALE = 1.0 / math.sqrt(DH)
EXP_C = SCALE * math.log2(math.e)


def rope_tables():
    freq = np.float32(500000.0) ** (-2.0 * np.arange(64, dtype=np.float32) / DH)
    freq = np.repeat(freq.astype(np.float64), 2)[None, :]
    sign = np.where(np.arange(DH) % 2 == 0, -1.0, 1.0)[None, :]
    fine = np.arange(128)[:, None] * freq
    coarse = 128 * np.arange(16)[:, None] * freq
    f = np.stack([np.cos(fine), np.sin(fine) * sign]).astype(np.float32)
    c = np.stack([np.cos(coarse), np.sin(coarse) * sign]).astype(np.float32)
    return f, c


def rope_block(fine_ref, coarse_ref, block):
    cf, sf = fine_ref[0], fine_ref[1]
    cc = coarse_ref[0, pl.ds(block, 1), :]
    sc = coarse_ref[1, pl.ds(block, 1), :]
    return cf * cc - sf * sc, sf * cc + cf * sc


def swap_pairs(x):
    lane = lax.broadcasted_iota(jnp.int32, x.shape, 1)
    return jnp.where(lane % 2 == 0, pltpu.roll(x, DH - 1, 1), pltpu.roll(x, 1, 1))


def nn(a, b):
    return jnp.dot(a, b, preferred_element_type=jnp.float32)


def nt(a, b):
    return lax.dot_general(a, b, (((1,), (1,)), ((), ())), preferred_element_type=jnp.float32)


def attention_kernel(qkv_ref, g_ref, docs_row, docs_col, fine_ref, coarse_ref,
                     att_ref, d_ref,
                     kt, vt, s_scr, p_scr, acc, dk_acc, dv_acc):
    bucket = lax.axis_index("bucket")
    q_ref, k_ref, v_ref = (qkv_ref.at[:, pl.ds(part * DH, DH)] for part in range(3))
    dq_ref, dk_ref, dv_ref = (d_ref.at[:, pl.ds(part * DH, DH)] for part in range(3))

    @pl.loop(0, SEQ // KB)
    def _(j):
        rows = pl.ds(pl.multiple_of(j * KB, KB), KB)
        kt[j] = k_ref[rows, :].T
        vt[j] = v_ref[rows, :].T

    dk_acc[...] = jnp.zeros_like(dk_acc)
    dv_acc[...] = jnp.zeros_like(dv_acc)

    def finish_query(i, dqt):
        dq = dqt.T * SCALE
        for half in range(QB // 128):
            block = i * (QB // 128) + half
            cos, sin = rope_block(fine_ref, coarse_ref, block)
            x = dq[half * 128:(half + 1) * 128]
            dq_ref[pl.ds(pl.multiple_of(block * 128, 128), 128), :] = (
                x * cos - swap_pairs(x) * sin).astype(jnp.bfloat16)

    @pl.when(bucket == 0)
    def _():
        @pl.loop(0, SEQ // QB)
        def _(i):
            qrows = pl.ds(pl.multiple_of(i * QB, QB), QB)
            q = q_ref[qrows, :]
            g = g_ref[qrows, :]

            def scores(j):
                return nt(k_ref[pl.ds(pl.multiple_of(j * KB, KB), KB), :], q)

            def pass1(j, m):
                s = scores(j)
                s_scr[j] = s
                return jnp.maximum(m, jnp.max(s.reshape(KB // 8, 8, QB), axis=0))

            m8 = lax.fori_loop(0, i, pass1, jnp.full((8, QB), NEG, jnp.float32))
            s = scores(i)
            key = lax.broadcasted_iota(jnp.int32, (KB, QB), 0)
            qry = lax.broadcasted_iota(jnp.int32, (KB, QB), 1)
            s = jnp.where(key <= qry, s, NEG)
            s_scr[i] = s
            m8 = jnp.maximum(m8, jnp.max(s.reshape(KB // 8, 8, QB), axis=0))
            m = jnp.max(m8, axis=0, keepdims=True)
            acc[...] = jnp.zeros_like(acc)

            def pass2(j, l8):
                p = jnp.exp2((s_scr[j] - m) * EXP_C)
                pb = p.astype(jnp.bfloat16)
                p_scr[j] = pb
                acc[...] += nn(vt[j], pb)
                return l8 + jnp.sum(p.reshape(KB // 8, 8, QB), axis=0)

            l8 = lax.fori_loop(0, i + 1, pass2, jnp.zeros((8, QB), jnp.float32))
            rl = 1.0 / jnp.sum(l8, axis=0, keepdims=True)
            ot = acc[...] * rl
            att_ref[qrows, :] = ot.T.astype(jnp.bfloat16)
            gt = (g.astype(jnp.float32).T * rl).astype(jnp.bfloat16)
            gs = gt.T
            d = jnp.sum(ot * gt.astype(jnp.float32), axis=0, keepdims=True)
            acc[...] = jnp.zeros_like(acc)

            @pl.loop(0, i + 1)
            def _(j):
                krows = pl.ds(pl.multiple_of(j * KB, KB), KB)
                pb = p_scr[j]
                dp = nn(v_ref[krows, :], gt)
                ds = (pb.astype(jnp.float32) * (dp - d)).astype(jnp.bfloat16)
                acc[...] += nn(kt[j], ds)
                dk_acc[krows, :] += nn(ds, q)
                dv_acc[krows, :] += nn(pb, gs)

            finish_query(i, acc[...])

    @pl.when(bucket == 1)
    def _():
        span = QB + 128

        @pl.loop(0, SEQ // QB)
        def _(i):
            qrows = pl.ds(pl.multiple_of(i * QB, QB), QB)
            first = pl.multiple_of(jnp.maximum(i * QB - 128, 0), 128)
            krows = pl.ds(first, span)
            q = q_ref[qrows, :]
            g = g_ref[qrows, :]
            k = k_ref[krows, :]
            v = v_ref[krows, :]
            key = lax.broadcasted_iota(jnp.int32, (span, QB), 0) + first
            qry = lax.broadcasted_iota(jnp.int32, (span, QB), 1) + i * QB
            same = docs_col[krows, :] == docs_row[i]
            s = jnp.where((key <= qry) & same, nt(k, q), NEG)
            m = jnp.max(s, axis=0, keepdims=True)
            p = jnp.exp2((s - m) * EXP_C)
            rl = 1.0 / jnp.sum(p, axis=0, keepdims=True)
            pb = p.astype(jnp.bfloat16)
            ot = nn(v.T, pb) * rl
            att_ref[qrows, :] = ot.T.astype(jnp.bfloat16)
            gt = (g.astype(jnp.float32).T * rl).astype(jnp.bfloat16)
            gs = gt.T
            d = jnp.sum(ot * gt.astype(jnp.float32), axis=0, keepdims=True)
            dp = nn(v, gt)
            ds = (pb.astype(jnp.float32) * (dp - d)).astype(jnp.bfloat16)
            finish_query(i, nn(k.T, ds))
            dk_acc[krows, :] += nn(ds, q)
            dv_acc[krows, :] += nn(pb, gs)

    dk_ref[...] = (dk_acc[...] * SCALE).astype(jnp.bfloat16)
    dv_ref[...] = dv_acc[...].astype(jnp.bfloat16)


def attention(qkv, g, docs, fine, coarse):
    nb = SEQ // KB
    vmem = pl.BlockSpec(memory_space=pltpu.VMEM)
    return pl.pallas_call(
        attention_kernel,
        out_shape=(jax.ShapeDtypeStruct((SEQ, DH), jnp.bfloat16), jax.ShapeDtypeStruct((SEQ, 3 * DH), jnp.bfloat16)),
        in_specs=[vmem] * 6,
        out_specs=(vmem,) * 2,
        scratch_shapes=[
            pltpu.VMEM((nb, DH, KB), jnp.bfloat16),
            pltpu.VMEM((nb, DH, KB), jnp.bfloat16),
            pltpu.VMEM((nb, KB, QB), jnp.float32),
            pltpu.VMEM((nb, KB, QB), jnp.bfloat16),
            pltpu.VMEM((DH, QB), jnp.float32),
            pltpu.VMEM((SEQ, DH), jnp.float32),
            pltpu.VMEM((SEQ, DH), jnp.float32),
        ],
        compiler_params=pltpu.CompilerParams(vmem_limit_bytes=40 << 20),
        name="attention",
    )(qkv, g, docs.reshape(SEQ // QB, 1, QB), docs.reshape(SEQ, 1), fine, coarse)


D = 4096
TB = 128
WR = 192
WF = 256
EPS = 1e-5


class Copies:
    def __init__(self, send, recv):
        self.send, self.recv, self.ids, self.live = send, recv, {}, []

    def make(self, key, src, dst, dev):
        i = self.ids.setdefault(key, len(self.ids))
        return pltpu.make_async_remote_copy(src_ref=src, dst_ref=dst, send_sem=self.send.at[i], recv_sem=self.recv.at[i],
                                            device_id=dev, device_id_type=MESH)

    def start(self, key, src, dst, dev):
        copy = self.make(key, src, dst, dev)
        copy.start()
        self.live.append(copy)

    def arrive(self, key, dst, dev):
        self.make(key, dst, dst, dev).wait_recv()

    def drain(self):
        for copy in self.live:
            copy.wait_send()


def place():
    c, z, sp = lax.axis_index("bucket"), lax.axis_index("fsdp"), lax.axis_index("sp")
    return c, z, sp // 4, sp % 4


def greet(devs):
    barrier = pltpu.get_barrier_semaphore()
    for dev in devs:
        pl.semaphore_signal(barrier, inc=1, device_id=dev, device_id_type=MESH)
    return lambda: pl.semaphore_wait(barrier, len(devs))


FRONT_SEMS = 7 + 32 + 32 + 12 + 12


def front_kernel(h_ref, gain_ref, w_ref, fine_ref, coarse_ref, n_ref, qkv_ref, wbuf, acc, stage, ssem, rsem):
    c, z, x, y = place()
    xdev = lambda d: {"sp": (x + d) % 4 * 4 + y}
    ydev = lambda d: {"sp": x * 4 + (y + d) % 4}
    zdev = lambda d: {"fsdp": (z + d) % 8}
    other = {"bucket": 1 - c}
    wait_all = greet([xdev(1), xdev(3), ydev(1), ydev(2), ydev(3), zdev(1), zdev(7), other])

    def wslot(core, zz, yy, lo=0, size=WR):
        col = pl.multiple_of((core * 8 + zz % 8) * WF, WF)
        return wbuf.at[yy % 4, pl.ds(lo, size), pl.ds(col, WF)]

    for r in range(0, TB, 32):
        rows = h_ref[r:r + 32, :].astype(jnp.float32)
        inv = lax.rsqrt(jnp.mean(rows * rows, axis=1, keepdims=True) + EPS)
        n_ref[x, r:r + 32, :] = (rows * inv * gain_ref[...]).astype(jnp.bfloat16)
    wslot(c, z, y)[...] = w_ref[...]
    wait_all()

    cp = Copies(ssem, rsem)
    zoff = [0, -1, -2, -3, -4, 1, 2, 3]

    def spread(zi):
        src = w_ref if zi == 0 else wslot(c, z + zoff[zi], y)
        dst = wslot(c, z + zoff[zi], y)
        cp.start(("yr", zi), src, dst, ydev(1))
        cp.start(("yl", zi), src, dst, ydev(3))
        cp.start(("c", zi, 0), src, dst, other)

    def serve(zi):
        zz = z + zoff[zi]
        cp.arrive(("yr", zi), wslot(c, zz, y + 3), ydev(1))
        half = wslot(c, zz, y + 3, 0, WR // 2)
        cp.start(("ya", zi), half, half, ydev(1))
        cp.start(("c", zi, 1), wslot(c, zz, y + 3), wslot(c, zz, y + 3), other)
        cp.arrive(("yl", zi), wslot(c, zz, y + 1), ydev(3))
        half = wslot(c, zz, y + 1, WR // 2, WR // 2)
        cp.start(("yb", zi), half, half, ydev(3))
        cp.start(("c", zi, 2), wslot(c, zz, y + 1), wslot(c, zz, y + 1), other)

    def last(zi):
        zz = z + zoff[zi]
        cp.arrive(("ya", zi), wslot(c, zz, y + 2, 0, WR // 2), ydev(1))
        cp.arrive(("yb", zi), wslot(c, zz, y + 2, WR // 2, WR // 2), ydev(3))
        cp.start(("c", zi, 3), wslot(c, zz, y + 2), wslot(c, zz, y + 2), other)

    def npiece(xx, p):
        return n_ref.at[xx % 4, pl.ds(p * 32, 32), :]

    cp.start(("zr", 1), w_ref, wslot(c, z, y), zdev(1))
    cp.start(("zl", 1), w_ref, wslot(c, z, y), zdev(7))
    spread(0)
    for p in range(4):
        cp.start(("xr", p), npiece(x, p), npiece(x, p), xdev(1))
        cp.start(("xl", 3 - p), npiece(x, 3 - p), npiece(x, 3 - p), xdev(3))

    def relay_x(p):
        cp.arrive(("xr", p), npiece(x + 3, p), xdev(1))
        cp.start(("xa", p), npiece(x + 3, p), npiece(x + 3, p), xdev(1))
        cp.arrive(("xl", 3 - p), npiece(x + 1, 3 - p), xdev(3))
        cp.start(("xb", 3 - p), npiece(x + 1, 3 - p), npiece(x + 1, 3 - p), xdev(3))

    done, waiting = [0], []
    for step in range(1, 5):
        src = wslot(c, z - step, y)
        cp.arrive(("zr", step), src, zdev(1))
        if step < 4:
            cp.start(("zr", step + 1), src, src, zdev(1))
        spread(step)
        fresh = [step]
        if step < 4:
            src = wslot(c, z + step, y)
            cp.arrive(("zl", step), src, zdev(7))
            if step < 3:
                cp.start(("zl", step + 1), src, src, zdev(7))
            spread(4 + step)
            fresh.append(4 + step)
        for zi in done:
            serve(zi)
        for zi in waiting:
            last(zi)
        waiting, done = done, fresh
        if step == 3:
            relay_x(0)
            relay_x(1)
    for zi in done:
        serve(zi)
    for zi in waiting + done:
        last(zi)
    for zi in range(8):
        for yk, dy in enumerate((0, 3, 1, 2)):
            cp.arrive(("c", zi, yk), wslot(1 - c, z + zoff[zi], y + dy), other)
    for p in (2, 3):
        cp.arrive(("xr", p), npiece(x + 3, p), xdev(1))
        cp.arrive(("xl", 3 - p), npiece(x + 1, 3 - p), xdev(3))

    lane = lax.broadcasted_iota(jnp.int32, (TB, DH), 1)

    def project(offsets, first):
        rows = len(offsets) * TB
        acc[0:rows, :] = jnp.zeros((rows, 6 * DH), jnp.float32)

        @pl.loop(0, D // 512)
        def _(f):
            cols = pl.ds(pl.multiple_of(f * 512, 512), 512)
            lhs = jnp.concatenate([n_ref[(x + d) % 4, :, cols] for d in offsets], axis=0)
            rhs = jnp.concatenate([wbuf[yy, 0:DH, cols] for yy in range(4)] + [wbuf[yy, DH:WR, cols] for yy in range(4)], axis=0)
            acc[0:rows, :] += nt(lhs, rhs)

        for n, d in enumerate(offsets):
            i = first + n
            xx = (x + d) % 4
            r = pl.ds(n * TB, TB)
            cos, sin = rope_block(fine_ref, coarse_ref, 4 * xx + y)
            turn = lambda t: (t * cos + swap_pairs(t) * sin).astype(jnp.bfloat16)
            a, b = acc[r, 4 * DH:5 * DH], acc[r, 5 * DH:6 * DH]
            pick = lambda p0, p1, p2, p3: jnp.where(lane < 32, p0, jnp.where(lane < 64, p1, jnp.where(lane < 96, p2, p3)))
            key = turn(pick(a, pltpu.roll(a, 96, 1), pltpu.roll(b, 64, 1), pltpu.roll(b, 32, 1)))
            val = pick(pltpu.roll(a, 96, 1), pltpu.roll(a, 64, 1), pltpu.roll(b, 32, 1), b).astype(jnp.bfloat16)
            for dy in range(4):
                q = turn(acc[r, pl.ds(pl.multiple_of((y + dy) % 4 * DH, DH), DH)])
                dst = qkv_ref.at[xx, y] if dy == 0 else stage.at[i, dy - 1]
                dst[:, 0:DH] = q
                dst[:, DH:2 * DH] = key
                dst[:, 2 * DH:3 * DH] = val
            for dy in (2, 1, 3):
                cp.start(("q", i, dy), stage.at[i, dy - 1], qkv_ref.at[xx, y], ydev(dy))

    project((0, 3, 1), 0)
    for p in (0, 1):
        cp.arrive(("xa", p), npiece(x + 2, p), xdev(1))
        cp.arrive(("xb", 3 - p), npiece(x + 2, 3 - p), xdev(3))
    project((2,), 3)
    for i, d in enumerate((0, 3, 1, 2)):
        for dy in range(1, 4):
            cp.arrive(("q", i, dy), qkv_ref.at[(x + d) % 4, (y - dy) % 4], ydev(dy))
    cp.drain()


def front(h, gain, w, fine, coarse):
    vmem = pl.BlockSpec(memory_space=pltpu.VMEM)
    return pl.pallas_call(
        front_kernel,
        out_shape=(jax.ShapeDtypeStruct((4, TB, D), jnp.bfloat16), jax.ShapeDtypeStruct((4, 4, TB, 3 * DH), jnp.bfloat16)),
        in_specs=[vmem] * 5,
        out_specs=(vmem,) * 2,
        scratch_shapes=[
            pltpu.VMEM((4, WR, D), jnp.bfloat16),
            pltpu.VMEM((3 * TB, 6 * DH), jnp.float32),
            pltpu.VMEM((4, 3, TB, 3 * DH), jnp.bfloat16),
            pltpu.SemaphoreType.DMA((FRONT_SEMS,)),
            pltpu.SemaphoreType.DMA((FRONT_SEMS,)),
        ],
        compiler_params=pltpu.CompilerParams(vmem_limit_bytes=40 << 20, collective_id=0, has_side_effects=True),
        name="front",
    )(h, gain, w, fine, coarse)


BACK_SEMS = 3 + 8 + 32 + 8


def back_kernel(n_ref, d_ref, fine_ref, coarse_ref, gq_ref, gk_ref, gv_ref,
                rbuf, dt, own, cstage, cbuf, hstage, hbuf, fstage, fbuf, zstage, zbuf, ssem, rsem):
    c, z, x, y = place()
    ydev = lambda d: {"sp": x * 4 + (y + d) % 4}
    zdev = lambda d: {"fsdp": (z + d) % 8}
    other = {"bucket": 1 - c}
    greet([ydev(1), ydev(2), ydev(3), other] + [zdev(d) for d in range(1, 8)])()
    cp = Copies(ssem, rsem)
    for dy in (2, 1, 3):
        cp.start(("d", dy), d_ref.at[:, (y + dy) % 4], rbuf.at[dy - 1], ydev(dy))
    for dy in range(1, 4):
        cp.arrive(("d", dy), rbuf.at[dy - 1], ydev(dy))

    for i in range(4):
        cols = pl.ds(i * TB, TB)
        part = [d_ref[i, y, :, :]] + [rbuf[dy - 1, i] for dy in range(1, 4)]
        for dy in range(4):
            dt[(y - dy) % 4, 0:DH, cols] = part[dy][:, 0:DH].T
        key, val = (sum(p[:, s * DH:(s + 1) * DH].astype(jnp.float32) for p in part) for s in (1, 2))
        cos, sin = rope_block(fine_ref, coarse_ref, 4 * i + y)
        key = (key * cos - swap_pairs(key) * sin).astype(jnp.bfloat16).T
        val = val.astype(jnp.bfloat16).T
        for yy in range(4):
            dt[yy, DH:DH + 32, cols] = key[yy * 32:(yy + 1) * 32]
            dt[yy, DH + 32:WR, cols] = val[yy * 32:(yy + 1) * 32]

    order = (4, 3, 5, 2, 6, 1, 7, 0)
    half = WR // 2

    def product(core, dz):
        col = pl.multiple_of((core * 8 + (z + dz) % 8) * WF, WF)
        rhs = n_ref[:, :, pl.ds(col, WF)].reshape(4 * TB, WF)
        return nn(dt[...].reshape(4 * WR, 4 * TB), rhs).reshape(4, WR, WF)

    def compute(t):
        cstage[t] = product(1 - c, order[t]).astype(jnp.bfloat16)
        cp.start(("c", t), cstage.at[t], cbuf.at[t], other)
        own[t] = product(c, order[t])

    def meet(t):
        cp.arrive(("c", t), cbuf.at[t], other)
        own[t] += cbuf[t].astype(jnp.float32)
        hstage[t, 0] = own[t, (y + 2) % 4, 0:half].astype(jnp.bfloat16)
        hstage[t, 1] = own[t, (y + 2) % 4, half:WR].astype(jnp.bfloat16)
        cp.start(("a", t), hstage.at[t, 0], hbuf.at[t, 0], ydev(1))
        cp.start(("b", t), hstage.at[t, 1], hbuf.at[t, 1], ydev(3))

    def pass_on(t):
        cp.arrive(("a", t), hbuf.at[t, 0], ydev(1))
        fstage[t, 0, 0:half] = (own[t, (y + 1) % 4, 0:half] + hbuf[t, 0].astype(jnp.float32)).astype(jnp.bfloat16)
        fstage[t, 0, half:WR] = own[t, (y + 1) % 4, half:WR].astype(jnp.bfloat16)
        cp.start(("r", t), fstage.at[t, 0], fbuf.at[t, 0], ydev(1))
        cp.arrive(("b", t), hbuf.at[t, 1], ydev(3))
        fstage[t, 1, 0:half] = own[t, (y + 3) % 4, 0:half].astype(jnp.bfloat16)
        fstage[t, 1, half:WR] = (own[t, (y + 3) % 4, half:WR] + hbuf[t, 1].astype(jnp.float32)).astype(jnp.bfloat16)
        cp.start(("l", t), fstage.at[t, 1], fbuf.at[t, 1], ydev(3))

    def home(t):
        cp.arrive(("r", t), fbuf.at[t, 0], ydev(1))
        cp.arrive(("l", t), fbuf.at[t, 1], ydev(3))
        total = own[t, y] + fbuf[t, 0].astype(jnp.float32) + fbuf[t, 1].astype(jnp.float32)
        if order[t] == 0:
            own[t, 0] = total
        else:
            zstage[t] = total.astype(jnp.bfloat16)
            cp.start(("z", t), zstage.at[t], zbuf.at[t], zdev(order[t]))

    for t in range(8 + 3):
        for delay, stage in ((0, compute), (1, meet), (2, pass_on), (3, home)):
            if 0 <= t - delay < 8:
                stage(t - delay)

    total = own[7, 0]
    for t in range(7):
        cp.arrive(("z", t), zbuf.at[t], zdev(order[t]))
        total = total + zbuf[t].astype(jnp.float32)
    gq_ref[...] = total[0:DH].T
    gk_ref[...] = total[DH:DH + 32].T
    gv_ref[...] = total[DH + 32:WR].T
    cp.drain()


def back(n, d, fine, coarse):
    vmem = pl.BlockSpec(memory_space=pltpu.VMEM)
    bf = jnp.bfloat16
    return pl.pallas_call(
        back_kernel,
        out_shape=tuple(jax.ShapeDtypeStruct((WF, w), jnp.float32) for w in (DH, 32, 32)),
        in_specs=[vmem] * 4,
        out_specs=(vmem,) * 3,
        scratch_shapes=[
            pltpu.VMEM((3, 4, TB, 3 * DH), bf),
            pltpu.VMEM((4, WR, 4 * TB), bf),
            pltpu.VMEM((8, 4, WR, WF), jnp.float32),
            pltpu.VMEM((8, 4, WR, WF), bf),
            pltpu.VMEM((8, 4, WR, WF), bf),
            pltpu.VMEM((8, 2, WR // 2, WF), bf),
            pltpu.VMEM((8, 2, WR // 2, WF), bf),
            pltpu.VMEM((8, 2, WR, WF), bf),
            pltpu.VMEM((8, 2, WR, WF), bf),
            pltpu.VMEM((7, WR, WF), bf),
            pltpu.VMEM((7, WR, WF), bf),
            pltpu.SemaphoreType.DMA((BACK_SEMS,)),
            pltpu.SemaphoreType.DMA((BACK_SEMS,)),
        ],
        compiler_params=pltpu.CompilerParams(vmem_limit_bytes=48 << 20, collective_id=1, has_side_effects=True),
        name="back",
    )(n, d, fine, coarse)


def local(hidden_states, norm_gain, w_query, w_key, w_value, out_grad, short_docs):
    fine, coarse = (jnp.asarray(t) for t in rope_tables())
    w = jnp.concatenate([w_query.T, w_key.T, w_value.T], axis=0)
    n, qkv = front(hidden_states.reshape(TB, D), norm_gain.reshape(1, D), w, fine, coarse)
    docs = jnp.where(lax.axis_index("bucket") == 0, 0, short_docs[0])
    att, d = attention(qkv.reshape(SEQ, 3 * DH), out_grad.reshape(SEQ, DH), docs, fine, coarse)
    gq, gk, gv = back(n, d.reshape(4, 4, TB, 3 * DH), fine, coarse)
    return att.reshape(1, 1, SEQ, DH), gq, gk, gv


def solution(mesh):
    both = ("bucket", "fsdp")
    return jax.shard_map(
        local,
        mesh=mesh,
        in_specs=(P("bucket", "fsdp", "sp", None), P(), P(both, "sp"), P(both, "sp"), P(both, "sp"),
                  P("bucket", "fsdp", None, "sp"), P("fsdp", None)),
        out_specs=(P("bucket", "fsdp", None, "sp"), P(both, "sp"), P(both, "sp"), P(both, "sp")),
        check_vma=False,
    )
```

time: 390 us -> 166 us (0.43)
  waiting for transfers between devices: 198 us -> 0 us
  Pallas kernels: 33.7 us -> 157 us
  blocking collectives: 58.7 us -> 0 us
  matrix products: 41.1 us -> 0 us
  other arithmetic: 17.7 us -> 0.78 us
  between operations: 14.1 us -> 0.72 us
  starting transfers between devices: 12.3 us -> 0 us
  local copies, waits for them, and re-layouts: 13.3 us -> 7.7 us
    pallas_call x1 -> x3, Pallas kernels: 33.7 us -> 157 us  [the longest x1 65.2 us: front(): pl.pallas_call(front_kernel, out_shape=(jax.ShapeDtypeStruct((4, TB, D),...]
    all_gather x2 -> x0, waiting for transfers between devices: 88.5 us -> none  [the longest x1 59.3 us: local(): normed = lax.all_gather(normed_local, 'sp', axis=0, tiled=True)]
    reduce_scatter x1 -> x0, waiting for transfers between devices: 62.8 us -> none  [local(): lax.psum_scatter(jnp.einsum('tc,tg->cg', columns, grads_joined, preferred...]
    all_gather x2 -> x0, blocking collectives: 58.7 us -> none  [the longest x1 30.3 us: local(): lax.all_gather(w_key, ('bucket', 'fsdp'), axis=0, tiled=True)]
    ppermute x8 -> x0, waiting for transfers between devices: 46.2 us -> none  [swapped(): return lax.ppermute(value, axis, pairs)]
    dot_general x4 -> x0, matrix products: 41.1 us -> none  [the longest x3 30.6 us: local(): jnp.dot(columns, piece, preferred_element_type=jnp.float32)]
    ppermute x8 -> x0, starting transfers between devices: 12.2 us -> none  [swapped(): return lax.ppermute(value, axis, pairs)]
    convert_element_type x4 -> x0, other arithmetic: 7.66 us -> none  [the longest x1 3.01 us: local(): dvalue = dvalue_cur.astype(jnp.bfloat16)]
  transfers between devices with their start and end apart: 11 -> 0, of which waited for: 11 -> 0; matrix products, arithmetic and copies ran while one was open for 8% -> 0% of each run, Pallas kernels for 0% -> 0%
where the time goes in v1:
time: 166 us
  Pallas kernels  157 us (95%)
  local copies, waits for them, and re-layouts  7.7 us (5%)
    pallas_call x1, Pallas kernels, front(): pl.pallas_call(front_kernel, out_shape=(jax.ShapeDtypeStruct((4, TB, D),...  65.2 us
    pallas_call x1, Pallas kernels, back(): pl.pallas_call(back_kernel, out_shape=tuple((jax.ShapeDtypeStruct((WF, w)...  57.4 us
    pallas_call x1, Pallas kernels, attention(): pl.pallas_call(attention_kernel, out_shape=(jax.ShapeDtypeStruct((SEQ, DH...  33.9 us
    unnamed x20, local copies, waits for them, and re-layouts  7.34 us

profile of v1, /device:TPU:2, one launch (start us, length us, event | category | flops | bytes accessed | tf_op | source)
XLA Modules:
  0.0 165.7 jit_solution(8765071193820052628)
XLA Ops:
  0.6 0.0 copy-start.3
  0.7 1.0 copy.16
  1.7 0.7 pad_maximum_fusion.w_ref
  2.5 0.4 copy.17.docs_col
  2.8 0.0 copy-done.3
  2.8 0.0 copy-start.1
  2.9 0.9 copy-done.1
  3.8 0.0 copy-start.5
  3.8 0.7 copy-done.5
  4.5 0.0 copy-start.7
  4.5 0.7 copy-done.7
  5.2 0.0 copy-start.4
  5.2 65.2 %front.1 = (bf16[4,128,4096]{2,1,0:T(8,128)(2,1)S(1)}, bf16[4,4,128,384]{3,2,1,0:T(8,128)(2,1)S(1)}) custom-call(bf16[128,4096]{1,0:T(8,128)(2,1)S(1)} %bitcast.14, f32[1,4096]{1,0:T(1,128)S(1)} %bitcast.17, bf16[192,256]{1,0:T(8,128)(2,1)S(1)} %pad_maximum_fusion.w_ref, f32[2,128,128]{2,1,0:T(8,128)S(1)} %copy-done.1, f32[2,16,128]{2,1,0:T(8,128)S(1)} %copy-done.5), custom_call_target="tpu_custom_call" | custom-call | tf_op jit(solution)/shard_map/front/pallas_call | solution.py:375
  70.4 0.0 copy-start
  70.4 1.9 %copy-done = bf16[4,128,4096]{2,1,0:T(8,128)(2,1)} copy-done((bf16[4,128,4096]{2,1,0:T(8,128)(2,1)}, bf16[4,128,4096]{2,1,0:T(8,128)(2,1)S(1)}, u32[]{:S(2)}) %copy-start) | copy-done | bytes 4194328
  72.3 0.0 copy-done.4
  72.3 0.0 copy-start.2
  72.3 0.0 copy-start.6
  72.3 33.9 %attention.1 = (bf16[2048,128]{1,0:T(8,128)(2,1)}, bf16[2048,384]{1,0:T(8,128)(2,1)S(1)}) custom-call(bf16[2048,384]{1,0:T(8,128)(2,1)S(1)} %bitcast.12, bf16[2048,128]{1,0:T(8,128)(2,1)S(1)} %bitcast.15, s32[8,1,256]{2,1,0:T(1,128)S(1)} %bitcast.16, s32[2048,1]{1,0:T(8,128)S(1)} %copy.17.docs_col, f32[2,128,128]{2,1,0:T(8,128)S(1)} %copy-done.1, ...), custom_call_target="tpu_custom_call" | custom-call | tf_op jit(solution)/shard_map/attention/pallas_call | solution.py:171
  106.3 0.0 copy-done.2
  106.3 0.0 copy-done.6
  106.3 57.4 %back.1 = (f32[256,128]{1,0:T(8,128)S(1)}, f32[256,32]{1,0:T(8,128)S(1)}, f32[256,32]{1,0:T(8,128)S(1)}) custom-call(bf16[4,128,4096]{2,1,0:T(8,128)(2,1)} %copy-done, bf16[4,4,128,384]{3,2,1,0:T(8,128)(2,1)S(1)} %bitcast.13, f32[2,128,128]{2,1,0:T(8,128)S(1)} %copy-done.2, f32[2,16,128]{2,1,0:T(8,128)S(1)} %copy-done.6), custom_call_target="tpu_custom_call" | custom-call | tf_op jit(solution)/shard_map/back/pallas_call | solution.py:480
  163.7 0.7 copy.18
  164.4 0.7 copy.19
  165.1 0.7 copy.21
  (2 shorter events, 0.0 us)
Async XLA Ops:
  0.6 2.2 %copy-start.3 = (bf16[1,1,128,4096]{3,2,1,0:T(8,128)(2,1)S(1)}, bf16[1,1,128,4096]{3,2,1,0:T(8,128)(2,1)}, u32[]{:S(2)}) copy-start(bf16[1,1,128,4096]{3,2,1,0:T(8,128)(2,1)} %param.9) | copy-start | bytes 3145732
  2.8 0.9 copy-start.1
  3.8 0.7 copy-start.5
  4.5 0.7 copy-start.7
  5.2 67.1 %copy-start.4 = (bf16[1,1,2048,128]{3,2,1,0:T(8,128)(2,1)S(1)}, bf16[1,1,2048,128]{3,2,1,0:T(8,128)(2,1)}, u32[]{:S(2)}) copy-start(bf16[1,1,2048,128]{3,2,1,0:T(8,128)(2,1)} %param.14) | copy-start | bytes 1572868
  70.4 1.9 %copy-start = (bf16[4,128,4096]{2,1,0:T(8,128)(2,1)}, bf16[4,128,4096]{2,1,0:T(8,128)(2,1)S(1)}, u32[]{:S(2)}) copy-start(bf16[4,128,4096]{2,1,0:T(8,128)(2,1)S(1)} %get-tuple-element.13.n_ref) | copy-start | bytes 12582916
  72.3 33.9 %copy-start.2 = (f32[2,128,128]{2,1,0:T(8,128)S(1)}, f32[2,128,128]{2,1,0:T(8,128)}, u32[]{:S(2)}) copy-start(f32[2,128,128]{2,1,0:T(8,128)} %constant.12.clone.fine_ref) | copy-start | bytes 393220
  72.3 33.9 %copy-start.6 = (f32[2,16,128]{2,1,0:T(8,128)S(1)}, f32[2,16,128]{2,1,0:T(8,128)}, u32[]{:S(2)}) copy-start(f32[2,16,128]{2,1,0:T(8,128)} %constant.13.clone.coarse_ref) | copy-start | bytes 49156

commit v2 on v0

v2 whole, which is shorter than its diff:
```python
import math
import functools
import numpy as np
import jax
import jax.numpy as jnp
from jax import lax
from jax.experimental import pallas as pl
from jax.experimental.pallas import tpu as pltpu
from jax.sharding import PartitionSpec as P

MESH = pl.DeviceIdType.MESH

DH = 128
SEQ = 2048
QB = 512
KB = 512
NEG = -1e30
SCALE = 1.0 / math.sqrt(DH)
EXP_C = SCALE * math.log2(math.e)


def rope_tables():
    freq = np.float32(500000.0) ** (-2.0 * np.arange(64, dtype=np.float32) / DH)
    freq = np.repeat(freq.astype(np.float64), 2)[None, :]
    sign = np.where(np.arange(DH) % 2 == 0, -1.0, 1.0)[None, :]
    fine = np.arange(128)[:, None] * freq
    coarse = 128 * np.arange(16)[:, None] * freq
    f = np.stack([np.cos(fine), np.sin(fine) * sign]).astype(np.float32)
    c = np.stack([np.cos(coarse), np.sin(coarse) * sign]).astype(np.float32)
    return f, c


def rope_block(fine_ref, coarse_ref, block):
    cf, sf = fine_ref[0], fine_ref[1]
    cc = coarse_ref[0, pl.ds(block, 1), :]
    sc = coarse_ref[1, pl.ds(block, 1), :]
    return cf * cc - sf * sc, sf * cc + cf * sc


def swap_pairs(x):
    lane = lax.broadcasted_iota(jnp.int32, x.shape, 1)
    return jnp.where(lane % 2 == 0, pltpu.roll(x, DH - 1, 1), pltpu.roll(x, 1, 1))


def nn(a, b):
    return jnp.dot(a, b, preferred_element_type=jnp.float32)


def nt(a, b):
    return lax.dot_general(a, b, (((1,), (1,)), ((), ())), preferred_element_type=jnp.float32)


D = 4096
TB = 128
WR = 192
WF = 256
EPS = 1e-5
RA, HA, HB = 112, 48, 32


class Copies:
    def __init__(self, send, recv):
        self.send, self.recv, self.ids, self.live = send, recv, {}, []

    def make(self, key, src, dst, dev):
        i = self.ids.setdefault(key, len(self.ids))
        return pltpu.make_async_remote_copy(src_ref=src, dst_ref=dst, send_sem=self.send.at[i], recv_sem=self.recv.at[i],
                                            device_id=dev, device_id_type=MESH)

    def start(self, key, src, dst, dev):
        copy = self.make(key, src, dst, dev)
        copy.start()
        self.live.append(copy)

    def arrive(self, key, dst, dev):
        self.make(key, dst, dst, dev).wait_recv()

    def drain(self):
        for copy in self.live:
            copy.wait_send()


def place():
    c, z, sp = lax.axis_index("bucket"), lax.axis_index("fsdp"), lax.axis_index("sp")
    return c, z, sp // 4, sp % 4


def greet(devs):
    barrier = pltpu.get_barrier_semaphore()
    for dev in devs:
        pl.semaphore_signal(barrier, inc=1, device_id=dev, device_id_type=MESH)
    return lambda: pl.semaphore_wait(barrier, len(devs))


FRONT_SEMS = 7 + 32 + 4 + 28 + 16 + 12 + 12


def front_kernel(h_ref, gain_ref, w_ref, fine_ref, coarse_ref, n_ref, qkv_ref, wbuf, acc, stage, ssem, rsem):
    c, z, x, y = place()
    xdev = lambda d: {"sp": (x + d) % 4 * 4 + y}
    ydev = lambda d: {"sp": x * 4 + (y + d) % 4}
    zdev = lambda d: {"fsdp": (z + d) % 8}
    other = {"bucket": 1 - c}
    wait_all = greet([xdev(1), xdev(3), ydev(1), ydev(2), ydev(3), zdev(1), zdev(7), other])

    def wslot(core, zz, yy, lo=0, size=WR):
        col = pl.multiple_of((core * 8 + zz % 8) * WF, WF)
        return wbuf.at[yy % 4, pl.ds(lo, size), pl.ds(col, WF)]

    for r in range(0, TB, 32):
        rows = h_ref[r:r + 32, :].astype(jnp.float32)
        inv = lax.rsqrt(jnp.mean(rows * rows, axis=1, keepdims=True) + EPS)
        n_ref[x, r:r + 32, :] = (rows * inv * gain_ref[...]).astype(jnp.bfloat16)
    wslot(c, z, y)[...] = w_ref[...]
    wait_all()

    cp = Copies(ssem, rsem)
    zoff = [0, -1, -2, -3, -4, 1, 2, 3]
    yoff = [0, 3, 1, 2]

    def spread(zi):
        src = w_ref.at[pl.ds(0, RA), :] if zi == 0 else wslot(c, z + zoff[zi], y, 0, RA)
        dst = wslot(c, z + zoff[zi], y, 0, RA)
        cp.start(("yr", zi), src, dst, ydev(1))
        cp.start(("yl", zi), src, dst, ydev(3))

    def serve(zi):
        zz = z + zoff[zi]
        cp.arrive(("yr", zi), wslot(c, zz, y + 3, 0, RA), ydev(1))
        part = wslot(c, zz, y + 3, 0, HA)
        cp.start(("ya", zi), part, part, ydev(1))
        cp.arrive(("yl", zi), wslot(c, zz, y + 1, 0, RA), ydev(3))
        part = wslot(c, zz, y + 1, HA, RA - HA)
        cp.start(("yb", zi), part, part, ydev(3))

    def wall(core, zz, lo, size):
        col = pl.multiple_of((core * 8 + zz % 8) * WF, WF)
        return wbuf.at[:, pl.ds(lo, size), pl.ds(col, WF)]

    def last(zi):
        zz = z + zoff[zi]
        cp.arrive(("ya", zi), wslot(c, zz, y + 2, 0, HA), ydev(1))
        cp.arrive(("yb", zi), wslot(c, zz, y + 2, HA, RA - HA), ydev(3))
        cp.start(("ca", zi), wall(c, zz, 0, RA), wall(c, zz, 0, RA), other)

    def chain(yk, step, right):
        n = 4 if right == (yk < 2) else 3
        if step > n:
            return
        zz = z - step if right else z + step
        name = "br" if right else "bl"
        part = wslot(c, zz, y + yoff[yk], RA, WR - RA)
        if step > 0:
            cp.arrive((name, yk, step), part, zdev(1 if right else 7))
        if step < n:
            src = w_ref.at[pl.ds(RA, WR - RA), :] if yk == 0 and step == 0 else part
            cp.start((name, yk, step + 1), src, part, zdev(1 if right else 7))

    def npiece(xx, p):
        return n_ref.at[xx % 4, pl.ds(p * 32, 32), :]

    own_a, own_b = w_ref.at[pl.ds(0, RA), :], w_ref.at[pl.ds(RA, WR - RA), :]
    cp.start(("zr", 1), own_a, wslot(c, z, y, 0, RA), zdev(1))
    cp.start(("zl", 1), own_a, wslot(c, z, y, 0, RA), zdev(7))
    cp.start(("er", 0), own_b, wslot(c, z, y, RA, WR - RA), ydev(1))
    cp.start(("el", 0), own_b, wslot(c, z, y, RA, WR - RA), ydev(3))
    spread(0)
    chain(0, 0, True)
    chain(0, 0, False)
    for p in range(4):
        cp.start(("xr", p), npiece(x, p), npiece(x, p), xdev(1))
        cp.start(("xl", 3 - p), npiece(x, 3 - p), npiece(x, 3 - p), xdev(3))
    cp.arrive(("er", 0), wslot(c, z, y + 3, RA, WR - RA), ydev(1))
    part = wslot(c, z, y + 3, RA, HB)
    cp.start(("ea", 0), part, part, ydev(1))
    chain(1, 0, True)
    chain(1, 0, False)
    cp.arrive(("el", 0), wslot(c, z, y + 1, RA, WR - RA), ydev(3))
    part = wslot(c, z, y + 1, RA + HB, WR - RA - HB)
    cp.start(("eb", 0), part, part, ydev(3))
    chain(2, 0, True)
    chain(2, 0, False)

    def relay_x(p):
        cp.arrive(("xr", p), npiece(x + 3, p), xdev(1))
        cp.start(("xa", p), npiece(x + 3, p), npiece(x + 3, p), xdev(1))
        cp.arrive(("xl", 3 - p), npiece(x + 1, 3 - p), xdev(3))
        cp.start(("xb", 3 - p), npiece(x + 1, 3 - p), npiece(x + 1, 3 - p), xdev(3))

    def core_b(zi):
        zz = z + zoff[zi]
        cp.start(("cb", zi), wall(c, zz, RA, WR - RA), wall(c, zz, RA, WR - RA), other)

    done, waiting = [0], []
    for step in range(1, 5):
        src = wslot(c, z - step, y, 0, RA)
        cp.arrive(("zr", step), src, zdev(1))
        if step < 4:
            cp.start(("zr", step + 1), src, src, zdev(1))
        spread(step)
        fresh = [step]
        if step < 4:
            src = wslot(c, z + step, y, 0, RA)
            cp.arrive(("zl", step), src, zdev(7))
            if step < 3:
                cp.start(("zl", step + 1), src, src, zdev(7))
            spread(4 + step)
            fresh.append(4 + step)
        if step == 1:
            cp.arrive(("ea", 0), wslot(c, z, y + 2, RA, HB), ydev(1))
            cp.arrive(("eb", 0), wslot(c, z, y + 2, RA + HB, WR - RA - HB), ydev(3))
            chain(3, 0, True)
            chain(3, 0, False)
            core_b(0)
        for zi in done:
            serve(zi)
        for yk in range(4):
            chain(yk, step, True)
            chain(yk, step, False)
        core_b(step)
        if step < 4:
            core_b(4 + step)
        for zi in waiting:
            last(zi)
        waiting, done = done, fresh
        if step == 3:
            relay_x(0)
            relay_x(1)
    for zi in done:
        serve(zi)
    for zi in waiting + done:
        last(zi)
    for zi in range(8):
        cp.arrive(("ca", zi), wall(1 - c, z + zoff[zi], 0, RA), other)
        cp.arrive(("cb", zi), wall(1 - c, z + zoff[zi], RA, WR - RA), other)

    lane = lax.broadcasted_iota(jnp.int32, (TB, DH), 1)

    def project(offsets, first):
        rows = len(offsets) * TB
        acc[0:rows, :] = jnp.zeros((rows, 6 * DH), jnp.float32)

        @pl.loop(0, D // 512)
        def _(f):
            cols = pl.ds(pl.multiple_of(f * 512, 512), 512)
            lhs = jnp.concatenate([n_ref[(x + d) % 4, :, cols] for d in offsets], axis=0)
            rhs = jnp.concatenate([wbuf[yy, 0:DH, cols] for yy in range(4)] + [wbuf[yy, DH:WR, cols] for yy in range(4)], axis=0)
            acc[0:rows, :] += nt(lhs, rhs)

        for n, d in enumerate(offsets):
            i = first + n
            xx = (x + d) % 4
            r = pl.ds(n * TB, TB)
            cos, sin = rope_block(fine_ref, coarse_ref, 4 * xx + y)
            turn = lambda t: (t * cos + swap_pairs(t) * sin).astype(jnp.bfloat16)
            a, b = acc[r, 4 * DH:5 * DH], acc[r, 5 * DH:6 * DH]
            pick = lambda p0, p1, p2, p3: jnp.where(lane < 32, p0, jnp.where(lane < 64, p1, jnp.where(lane < 96, p2, p3)))
            key = turn(pick(a, pltpu.roll(a, 96, 1), pltpu.roll(b, 64, 1), pltpu.roll(b, 32, 1)))
            val = pick(pltpu.roll(a, 96, 1), pltpu.roll(a, 64, 1), pltpu.roll(b, 32, 1), b).astype(jnp.bfloat16)
            for dy in range(4):
                q = turn(acc[r, pl.ds(pl.multiple_of((y + dy) % 4 * DH, DH), DH)])
                dst = qkv_ref.at[xx, y] if dy == 0 else stage.at[i, dy - 1]
                dst[:, 0:DH] = q
                dst[:, DH:2 * DH] = key
                dst[:, 2 * DH:3 * DH] = val
            for dy in (2, 1, 3):
                cp.start(("q", i, dy), stage.at[i, dy - 1], qkv_ref.at[xx, y], ydev(dy))

    project((0,), 0)
    for p in (2, 3):
        cp.arrive(("xr", p), npiece(x + 3, p), xdev(1))
        cp.arrive(("xl", 3 - p), npiece(x + 1, 3 - p), xdev(3))
    project((3, 1), 1)
    for p in (0, 1):
        cp.arrive(("xa", p), npiece(x + 2, p), xdev(1))
        cp.arrive(("xb", 3 - p), npiece(x + 2, 3 - p), xdev(3))
    project((2,), 3)
    for i, d in enumerate((0, 3, 1, 2)):
        for dy in range(1, 4):
            cp.arrive(("q", i, dy), qkv_ref.at[(x + d) % 4, (y - dy) % 4], ydev(dy))
    cp.drain()


def front(h, gain, w, fine, coarse):
    vmem = pl.BlockSpec(memory_space=pltpu.VMEM)
    return pl.pallas_call(
        front_kernel,
        out_shape=(jax.ShapeDtypeStruct((4, TB, D), jnp.bfloat16), jax.ShapeDtypeStruct((4, 4, TB, 3 * DH), jnp.bfloat16)),
        in_specs=[vmem] * 5,
        out_specs=(vmem,) * 2,
        scratch_shapes=[
            pltpu.VMEM((4, WR, D), jnp.bfloat16),
            pltpu.VMEM((3 * TB, 6 * DH), jnp.float32),
            pltpu.VMEM((4, 3, TB, 3 * DH), jnp.bfloat16),
            pltpu.SemaphoreType.DMA((FRONT_SEMS,)),
            pltpu.SemaphoreType.DMA((FRONT_SEMS,)),
        ],
        compiler_params=pltpu.CompilerParams(vmem_limit_bytes=40 << 20, collective_id=0, has_side_effects=True),
        name="front",
    )(h, gain, w, fine, coarse)


TAIL_SEMS = 8 + 32 + 7


def tail_kernel(qkv_ref, g_ref, docs_row, docs_col, n_ref, fine_ref, coarse_ref, att_ref, gq_ref, gk_ref, gv_ref,
                kt, vt, s_scr, p_scr, acc, dk_acc, dv_acc, d_scr, dsend, drecv,
                rbuf, dt, own, cstage, cbuf, hstage, hbuf, fstage, fbuf, zstage, zbuf, ssem, rsem):
    c, z, x, y = place()
    ydev = lambda d: {"sp": x * 4 + (y + d) % 4}
    zdev = lambda d: {"fsdp": (z + d) % 8}
    other = {"bucket": 1 - c}
    greet([ydev(1), ydev(2), ydev(3), other] + [zdev(d) for d in range(1, 8)])()
    cp = Copies(ssem, rsem)
    q_ref, k_ref, v_ref = (qkv_ref.at[:, pl.ds(part * DH, DH)] for part in range(3))

    def exchange(i, dy):
        return pltpu.make_async_remote_copy(
            src_ref=d_scr.at[i, (y + dy) % 4], dst_ref=rbuf.at[dy - 1, i], send_sem=dsend.at[i, dy - 1],
            recv_sem=drecv.at[i, dy - 1], device_id=ydev(dy), device_id_type=MESH)

    @pl.loop(0, SEQ // KB)
    def _(j):
        rows = pl.ds(pl.multiple_of(j * KB, KB), KB)
        kt[j] = k_ref[rows, :].T
        vt[j] = v_ref[rows, :].T

    dk_acc[...] = jnp.zeros_like(dk_acc)
    dv_acc[...] = jnp.zeros_like(dv_acc)

    def finish_query(i, dqt):
        dq = dqt.T * SCALE
        for half in range(QB // 128):
            block = i * (QB // 128) + half
            cos, sin = rope_block(fine_ref, coarse_ref, block)
            x = dq[half * 128:(half + 1) * 128]
            rows = pl.ds(pl.multiple_of(block * 128, 128), 128)
            d_scr[i, half, :, 0:DH] = (x * cos - swap_pairs(x) * sin).astype(jnp.bfloat16)
            d_scr[i, half, :, DH:2 * DH] = (dk_acc[rows, :] * SCALE).astype(jnp.bfloat16)
            d_scr[i, half, :, 2 * DH:3 * DH] = dv_acc[rows, :].astype(jnp.bfloat16)
        for dy in (2, 1, 3):
            exchange(i, dy).start()

    @pl.when(c == 0)
    def _():
        @pl.loop(0, SEQ // QB)
        def _(step):
            i = SEQ // QB - 1 - step
            qrows = pl.ds(pl.multiple_of(i * QB, QB), QB)
            q = q_ref[qrows, :]
            g = g_ref[qrows, :]

            def scores(j):
                return nt(k_ref[pl.ds(pl.multiple_of(j * KB, KB), KB), :], q)

            def pass1(j, m):
                s = scores(j)
                s_scr[j] = s
                return jnp.maximum(m, jnp.max(s.reshape(KB // 8, 8, QB), axis=0))

            m8 = lax.fori_loop(0, i, pass1, jnp.full((8, QB), NEG, jnp.float32))
            s = scores(i)
            key = lax.broadcasted_iota(jnp.int32, (KB, QB), 0)
            qry = lax.broadcasted_iota(jnp.int32, (KB, QB), 1)
            s = jnp.where(key <= qry, s, NEG)
            s_scr[i] = s
            m8 = jnp.maximum(m8, jnp.max(s.reshape(KB // 8, 8, QB), axis=0))
            m = jnp.max(m8, axis=0, keepdims=True)
            acc[...] = jnp.zeros_like(acc)

            def pass2(j, l8):
                p = jnp.exp2((s_scr[j] - m) * EXP_C)
                pb = p.astype(jnp.bfloat16)
                p_scr[j] = pb
                acc[...] += nn(vt[j], pb)
                return l8 + jnp.sum(p.reshape(KB // 8, 8, QB), axis=0)

            l8 = lax.fori_loop(0, i + 1, pass2, jnp.zeros((8, QB), jnp.float32))
            rl = 1.0 / jnp.sum(l8, axis=0, keepdims=True)
            ot = acc[...] * rl
            att_ref[qrows, :] = ot.T.astype(jnp.bfloat16)
            gt = (g.astype(jnp.float32).T * rl).astype(jnp.bfloat16)
            gs = gt.T
            d = jnp.sum(ot * gt.astype(jnp.float32), axis=0, keepdims=True)
            acc[...] = jnp.zeros_like(acc)

            @pl.loop(0, i + 1)
            def _(j):
                krows = pl.ds(pl.multiple_of(j * KB, KB), KB)
                pb = p_scr[j]
                dp = nn(v_ref[krows, :], gt)
                ds = (pb.astype(jnp.float32) * (dp - d)).astype(jnp.bfloat16)
                acc[...] += nn(kt[j], ds)
                dk_acc[krows, :] += nn(ds, q)
                dv_acc[krows, :] += nn(pb, gs)

            finish_query(i, acc[...])

    @pl.when(c == 1)
    def _():
        span = QB + 128

        @pl.loop(0, SEQ // QB)
        def _(step):
            i = SEQ // QB - 1 - step
            qrows = pl.ds(pl.multiple_of(i * QB, QB), QB)
            first = pl.multiple_of(jnp.maximum(i * QB - 128, 0), 128)
            krows = pl.ds(first, span)
            q = q_ref[qrows, :]
            g = g_ref[qrows, :]
            k = k_ref[krows, :]
            v = v_ref[krows, :]
            key = lax.broadcasted_iota(jnp.int32, (span, QB), 0) + first
            qry = lax.broadcasted_iota(jnp.int32, (span, QB), 1) + i * QB
            same = docs_col[krows, :] == docs_row[i]
            s = jnp.where((key <= qry) & same, nt(k, q), NEG)
            m = jnp.max(s, axis=0, keepdims=True)
            p = jnp.exp2((s - m) * EXP_C)
            rl = 1.0 / jnp.sum(p, axis=0, keepdims=True)
            pb = p.astype(jnp.bfloat16)
            ot = nn(v.T, pb) * rl
            att_ref[qrows, :] = ot.T.astype(jnp.bfloat16)
            gt = (g.astype(jnp.float32).T * rl).astype(jnp.bfloat16)
            gs = gt.T
            d = jnp.sum(ot * gt.astype(jnp.float32), axis=0, keepdims=True)
            dp = nn(v, gt)
            ds = (pb.astype(jnp.float32) * (dp - d)).astype(jnp.bfloat16)
            dk_acc[krows, :] += nn(ds, q)
            dv_acc[krows, :] += nn(pb, gs)
            finish_query(i, nn(k.T, ds))

    for i in (3, 2, 1, 0):
        for dy in range(1, 4):
            exchange(i, dy).wait()

    for i in range(4):
        cols = pl.ds(i * TB, TB)
        part = [d_scr[i, y]] + [rbuf[dy - 1, i] for dy in range(1, 4)]
        for dy in range(4):
            dt[(y - dy) % 4, 0:DH, cols] = part[dy][:, 0:DH].T
        key, val = (sum(p[:, s * DH:(s + 1) * DH].astype(jnp.float32) for p in part) for s in (1, 2))
        cos, sin = rope_block(fine_ref, coarse_ref, 4 * i + y)
        key = (key * cos - swap_pairs(key) * sin).astype(jnp.bfloat16).T
        val = val.astype(jnp.bfloat16).T
        for yy in range(4):
            dt[yy, DH:DH + 32, cols] = key[yy * 32:(yy + 1) * 32]
            dt[yy, DH + 32:WR, cols] = val[yy * 32:(yy + 1) * 32]

    order = (4, 3, 5, 2, 6, 1, 7, 0)
    half = WR // 2

    def product(core, dz):
        col = pl.multiple_of((core * 8 + (z + dz) % 8) * WF, WF)
        rhs = n_ref[:, :, pl.ds(col, WF)].reshape(4 * TB, WF)
        return nn(dt[...].reshape(4 * WR, 4 * TB), rhs).reshape(4, WR, WF)

    def compute(t):
        cstage[t] = product(1 - c, order[t]).astype(jnp.bfloat16)
        cp.start(("c", t), cstage.at[t], cbuf.at[t], other)
        own[t] = product(c, order[t])

    def meet(t):
        cp.arrive(("c", t), cbuf.at[t], other)
        own[t] += cbuf[t].astype(jnp.float32)
        hstage[t, 0] = own[t, (y + 2) % 4, 0:half].astype(jnp.bfloat16)
        hstage[t, 1] = own[t, (y + 2) % 4, half:WR].astype(jnp.bfloat16)
        cp.start(("a", t), hstage.at[t, 0], hbuf.at[t, 0], ydev(1))
        cp.start(("b", t), hstage.at[t, 1], hbuf.at[t, 1], ydev(3))

    def pass_on(t):
        cp.arrive(("a", t), hbuf.at[t, 0], ydev(1))
        fstage[t, 0, 0:half] = (own[t, (y + 1) % 4, 0:half] + hbuf[t, 0].astype(jnp.float32)).astype(jnp.bfloat16)
        fstage[t, 0, half:WR] = own[t, (y + 1) % 4, half:WR].astype(jnp.bfloat16)
        cp.start(("r", t), fstage.at[t, 0], fbuf.at[t, 0], ydev(1))
        cp.arrive(("b", t), hbuf.at[t, 1], ydev(3))
        fstage[t, 1, 0:half] = own[t, (y + 3) % 4, 0:half].astype(jnp.bfloat16)
        fstage[t, 1, half:WR] = (own[t, (y + 3) % 4, half:WR] + hbuf[t, 1].astype(jnp.float32)).astype(jnp.bfloat16)
        cp.start(("l", t), fstage.at[t, 1], fbuf.at[t, 1], ydev(3))

    def home(t):
        cp.arrive(("r", t), fbuf.at[t, 0], ydev(1))
        cp.arrive(("l", t), fbuf.at[t, 1], ydev(3))
        total = own[t, y] + fbuf[t, 0].astype(jnp.float32) + fbuf[t, 1].astype(jnp.float32)
        if order[t] == 0:
            own[t, 0] = total
        else:
            zstage[t] = total.astype(jnp.bfloat16)
            cp.start(("z", t), zstage.at[t], zbuf.at[t], zdev(order[t]))

    for t in range(8 + 3):
        for delay, stage in ((0, compute), (1, meet), (2, pass_on), (3, home)):
            if 0 <= t - delay < 8:
                stage(t - delay)

    total = own[7, 0]
    for t in range(7):
        cp.arrive(("z", t), zbuf.at[t], zdev(order[t]))
        total = total + zbuf[t].astype(jnp.float32)
    gq_ref[...] = total[0:DH].T
    gk_ref[...] = total[DH:DH + 32].T
    gv_ref[...] = total[DH + 32:WR].T
    cp.drain()


def tail(qkv, g, docs, n, fine, coarse):
    vmem = pl.BlockSpec(memory_space=pltpu.VMEM)
    bf, f32, nb = jnp.bfloat16, jnp.float32, SEQ // KB
    return pl.pallas_call(
        tail_kernel,
        out_shape=(jax.ShapeDtypeStruct((SEQ, DH), bf),) + tuple(jax.ShapeDtypeStruct((WF, w), f32) for w in (DH, 32, 32)),
        in_specs=[vmem] * 7,
        out_specs=(vmem,) * 4,
        scratch_shapes=[
            pltpu.VMEM((nb, DH, KB), bf),
            pltpu.VMEM((nb, DH, KB), bf),
            pltpu.VMEM((nb, KB, QB), f32),
            pltpu.VMEM((nb, KB, QB), bf),
            pltpu.VMEM((DH, QB), f32),
            pltpu.VMEM((SEQ, DH), f32),
            pltpu.VMEM((SEQ, DH), f32),
            pltpu.VMEM((4, 4, TB, 3 * DH), bf),
            pltpu.SemaphoreType.DMA((4, 3)),
            pltpu.SemaphoreType.DMA((4, 3)),
            pltpu.VMEM((3, 4, TB, 3 * DH), bf),
            pltpu.VMEM((4, WR, 4 * TB), bf),
            pltpu.VMEM((8, 4, WR, WF), f32),
            pltpu.VMEM((8, 4, WR, WF), bf),
            pltpu.VMEM((8, 4, WR, WF), bf),
            pltpu.VMEM((8, 2, WR // 2, WF), bf),
            pltpu.VMEM((8, 2, WR // 2, WF), bf),
            pltpu.VMEM((8, 2, WR, WF), bf),
            pltpu.VMEM((8, 2, WR, WF), bf),
            pltpu.VMEM((7, WR, WF), bf),
            pltpu.VMEM((7, WR, WF), bf),
            pltpu.SemaphoreType.DMA((TAIL_SEMS,)),
            pltpu.SemaphoreType.DMA((TAIL_SEMS,)),
        ],
        compiler_params=pltpu.CompilerParams(vmem_limit_bytes=56 << 20, collective_id=1, has_side_effects=True),
        name="tail",
    )(qkv, g, docs.reshape(SEQ // QB, 1, QB), docs.reshape(SEQ, 1), n, fine, coarse)


def local(hidden_states, norm_gain, w_query, w_key, w_value, out_grad, short_docs):
    fine, coarse = (jnp.asarray(t) for t in rope_tables())
    w = jnp.concatenate([w_query.T, w_key.T, w_value.T], axis=0)
    n, qkv = front(hidden_states.reshape(TB, D), norm_gain.reshape(1, D), w, fine, coarse)
    docs = jnp.where(lax.axis_index("bucket") == 0, 0, short_docs[0])
    att, gq, gk, gv = tail(qkv.reshape(SEQ, 3 * DH), out_grad.reshape(SEQ, DH), docs, n, fine, coarse)
    return att.reshape(1, 1, SEQ, DH), gq, gk, gv


def solution(mesh):
    both = ("bucket", "fsdp")
    return jax.shard_map(
        local,
        mesh=mesh,
        in_specs=(P("bucket", "fsdp", "sp", None), P(), P(both, "sp"), P(both, "sp"), P(both, "sp"),
                  P("bucket", "fsdp", None, "sp"), P("fsdp", None)),
        out_specs=(P("bucket", "fsdp", None, "sp"), P(both, "sp"), P(both, "sp"), P(both, "sp")),
        check_vma=False,
    )
```

time: 390 us -> 144 us (0.37)
  waiting for transfers between devices: 198 us -> 0 us
  Pallas kernels: 33.7 us -> 125 us
  blocking collectives: 58.7 us -> 0 us
  matrix products: 41.1 us -> 0 us
  other arithmetic: 17.7 us -> 1.38 us
  between operations: 14.1 us -> 0.68 us
  starting transfers between devices: 12.3 us -> 0 us
    pallas_call x1 -> x2, Pallas kernels: 33.7 us -> 125 us  [the longest x1 64.7 us: tail(): pl.pallas_call(tail_kernel, out_shape=(jax.ShapeDtypeStruct((SEQ, DH), bf...]
    all_gather x2 -> x0, waiting for transfers between devices: 88.5 us -> none  [the longest x1 59.3 us: local(): normed = lax.all_gather(normed_local, 'sp', axis=0, tiled=True)]
    reduce_scatter x1 -> x0, waiting for transfers between devices: 62.8 us -> none  [local(): lax.psum_scatter(jnp.einsum('tc,tg->cg', columns, grads_joined, preferred...]
    all_gather x2 -> x0, blocking collectives: 58.7 us -> none  [the longest x1 30.3 us: local(): lax.all_gather(w_key, ('bucket', 'fsdp'), axis=0, tiled=True)]
    ppermute x8 -> x0, waiting for transfers between devices: 46.2 us -> none  [swapped(): return lax.ppermute(value, axis, pairs)]
    dot_general x4 -> x0, matrix products: 41.1 us -> none  [the longest x3 30.6 us: local(): jnp.dot(columns, piece, preferred_element_type=jnp.float32)]
    unnamed x17, local copies, waits for them, and re-layouts: 1.62 us -> 14.2 us
    ppermute x8 -> x0, starting transfers between devices: 12.2 us -> none  [swapped(): return lax.ppermute(value, axis, pairs)]
  transfers between devices with their start and end apart: 11 -> 0, of which waited for: 11 -> 0; matrix products, arithmetic and copies ran while one was open for 8% -> 0% of each run, Pallas kernels for 0% -> 0%
where the time goes in v2:
time: 144 us; the launch traced here: 143 us
  Pallas kernels  125 us (87%)
  local copies, waits for them, and re-layouts  15.6 us (11%)
    pallas_call x1, Pallas kernels, tail(): pl.pallas_call(tail_kernel, out_shape=(jax.ShapeDtypeStruct((SEQ, DH), bf...  64.7 us
    pallas_call x1, Pallas kernels, front(): pl.pallas_call(front_kernel, out_shape=(jax.ShapeDtypeStruct((4, TB, D),...  60.7 us
    unnamed x17, local copies, waits for them, and re-layouts  14.2 us

profile of v2, /device:TPU:2, one launch (start us, length us, event | category | flops | bytes accessed | tf_op | source)
XLA Modules:
  0.0 143.0 jit_solution(6971729838688660221)
XLA Ops:
  0.7 0.6 broadcast_select_fusion
  1.3 0.9 copy.16
  2.2 0.7 pad_maximum_fusion.w_ref
  3.0 1.4 copy.17.docs_col
  4.4 0.0 copy-start.2
  4.4 1.2 copy-done.2
  5.6 0.0 copy-start.3
  5.6 0.9 copy-done.3
  6.5 0.0 copy-start.4
  6.5 0.7 copy-done.4
  7.2 0.0 copy-start.5
  7.2 0.7 copy-done.5
  7.9 60.7 %front.1 = (bf16[4,128,4096]{2,1,0:T(8,128)(2,1)S(1)}, bf16[4,4,128,384]{3,2,1,0:T(8,128)(2,1)S(1)}) custom-call(bf16[128,4096]{1,0:T(8,128)(2,1)S(1)} %bitcast.12, f32[1,4096]{1,0:T(1,128)S(1)} %bitcast.13, bf16[192,256]{1,0:T(8,128)(2,1)S(1)} %pad_maximum_fusion.w_ref, f32[2,128,128]{2,1,0:T(8,128)S(1)} %copy-done.3, f32[2,16,128]{2,1,0:T(8,128)S(1)} %copy-done.4), custom_call_target="tpu_custom_call" | custom-call | tf_op jit(solution)/shard_map/front/pallas_call | solution.py:286
  68.6 0.0 copy-start
  68.6 1.9 %copy-done = bf16[4,128,4096]{2,1,0:T(8,128)(2,1)} copy-done((bf16[4,128,4096]{2,1,0:T(8,128)(2,1)}, bf16[4,128,4096]{2,1,0:T(8,128)(2,1)S(1)}, u32[]{:S(2)}) %copy-start) | copy-done | bytes 4194328
  70.6 0.0 copy-start.1
  70.6 1.2 copy-done.1
  71.7 64.7 %tail.1 = (bf16[2048,128]{1,0:T(8,128)(2,1)}, f32[256,128]{1,0:T(8,128)}, f32[256,32]{1,0:T(8,128)}, f32[256,32]{1,0:T(8,128)}) custom-call(bf16[2048,384]{1,0:T(8,128)(2,1)} %bitcast.11, bf16[2048,128]{1,0:T(8,128)(2,1)} %bitcast.14, s32[4,1,512]{2,1,0:T(1,128)} %bitcast.17, s32[2048,1]{1,0:T(8,128)} %copy.17.docs_col, bf16[4,128,4096]{2,1,0:T(8,128)(2,1)} %copy-done, ...), custom_call_target="tpu_custom_call" | custom-call | tf_op jit(solution)/shard_map/tail/pallas_call | solution.py:508
  136.4 1.6 %copy.18 = f32[256,32]{0,1:T(8,128)} copy(f32[256,32]{1,0:T(8,128)} %get-tuple-element.22) | data formatting | bytes 65536
  138.0 1.6 %copy.19 = f32[256,32]{0,1:T(8,128)} copy(f32[256,32]{1,0:T(8,128)} %get-tuple-element.23) | data formatting | bytes 65536
  139.6 1.9 %copy.22 = bf16[1,1,2048,128]{3,2,1,0:T(8,128)(2,1)} copy(bf16[1,1,2048,128]{3,2,1,0:T(8,128)(2,1)} %bitcast.15) | data formatting | bytes 1048576
  141.5 1.6 %copy.23 = f32[256,128]{1,0:T(8,128)} copy(f32[256,128]{1,0:T(8,128)} %get-tuple-element.29) | data formatting | bytes 262144
  (1 shorter events, 0.0 us)
Async XLA Ops:
  4.4 1.2 copy-start.2
  5.6 0.9 copy-start.3
  6.5 0.7 copy-start.4
  7.2 0.7 copy-start.5
  68.6 1.9 %copy-start = (bf16[4,128,4096]{2,1,0:T(8,128)(2,1)}, bf16[4,128,4096]{2,1,0:T(8,128)(2,1)S(1)}, u32[]{:S(2)}) copy-start(bf16[4,128,4096]{2,1,0:T(8,128)(2,1)S(1)} %get-tuple-element.11.n_ref) | copy-start | bytes 12582916
  70.6 1.2 copy-start.1

commit v3 on v2

--- a/solution.py
+++ b/solution.py
@@ -92,28 +92,48 @@
     return lambda: pl.semaphore_wait(barrier, len(devs))
 
 
-FRONT_SEMS = 7 + 32 + 4 + 28 + 16 + 12 + 12
-
-
-def front_kernel(h_ref, gain_ref, w_ref, fine_ref, coarse_ref, n_ref, qkv_ref, wbuf, acc, stage, ssem, rsem):
+SEMS = 7 + 32 + 4 + 28 + 16 + 12 + 12 + 8 + 32 + 7
+
+
+class Part:
+    def __init__(self, ref, part):
+        self.ref, self.part = ref, part
+
+    def __getitem__(self, index):
+        return self.ref[index[0], self.part * DH:(self.part + 1) * DH]
+
+
+def block_kernel(h_hbm, gain_hbm, wq_hbm, wk_hbm, wv_hbm, g_hbm, docs_hbm, fine_hbm, coarse_hbm, att_ref, grad_ref,
+                 h_ref, gain_ref, wq_ref, wk_ref, wv_ref, g_ref, docs_ref, fine_ref, coarse_ref, w_ref,
+                 n_ref, qkv4_ref, wbuf, pacc, stage,
+                 kt, vt, s_scr, p_scr, acc, dk_acc, dv_acc, d_scr, dsend, drecv,
+                 rbuf, dt, own, cstage, cbuf, hstage, hbuf, fstage, fbuf, zstage, zbuf, ssem, rsem, lsem):
+    loads = {}
+    for name, src, dst in (("wq", wq_hbm, wq_ref), ("wk", wk_hbm, wk_ref), ("wv", wv_hbm, wv_ref), ("h", h_hbm, h_ref),
+                           ("gain", gain_hbm, gain_ref), ("fine", fine_hbm, fine_ref), ("coarse", coarse_hbm, coarse_ref),
+                           ("g", g_hbm, g_ref), ("docs", docs_hbm, docs_ref)):
+        loads[name] = pltpu.make_async_copy(src, dst, lsem.at[len(loads)])
+        loads[name].start()
     c, z, x, y = place()
     xdev = lambda d: {"sp": (x + d) % 4 * 4 + y}
     ydev = lambda d: {"sp": x * 4 + (y + d) % 4}
     zdev = lambda d: {"fsdp": (z + d) % 8}
     other = {"bucket": 1 - c}
-    wait_all = greet([xdev(1), xdev(3), ydev(1), ydev(2), ydev(3), zdev(1), zdev(7), other])
+    wait_all = greet([xdev(1), xdev(3), ydev(1), ydev(2), ydev(3), other] + [zdev(d) for d in range(1, 8)])
+    qkv_ref = qkv4_ref
 
     def wslot(core, zz, yy, lo=0, size=WR):
         col = pl.multiple_of((core * 8 + zz % 8) * WF, WF)
         return wbuf.at[yy % 4, pl.ds(lo, size), pl.ds(col, WF)]
 
-    for r in range(0, TB, 32):
-        rows = h_ref[r:r + 32, :].astype(jnp.float32)
-        inv = lax.rsqrt(jnp.mean(rows * rows, axis=1, keepdims=True) + EPS)
-        n_ref[x, r:r + 32, :] = (rows * inv * gain_ref[...]).astype(jnp.bfloat16)
+    for name in ("wq", "wk", "wv"):
+        loads[name].wait()
+    w_ref[0:DH] = wq_ref[...].T
+    w_ref[DH:DH + 32] = wk_ref[...].T
+    w_ref[DH + 32:WR] = wv_ref[...].T
     wslot(c, z, y)[...] = w_ref[...]
     wait_all()
-
+    loads["gain"].wait()
     cp = Copies(ssem, rsem)
     zoff = [0, -1, -2, -3, -4, 1, 2, 3]
     yoff = [0, 3, 1, 2]
@@ -167,7 +187,16 @@
     spread(0)
     chain(0, 0, True)
     chain(0, 0, False)
-    for p in range(4):
+    loads["h"].wait()
+    for p in (0, 3, 1, 2):
+        rows = h_ref[p * 32:(p + 1) * 32, :].astype(jnp.float32)
+        inv = lax.rsqrt(jnp.mean(rows * rows, axis=1, keepdims=True) + EPS)
+        n_ref[x, p * 32:(p + 1) * 32, :] = (rows * inv * gain_ref[...]).astype(jnp.bfloat16)
+        if p in (0, 1):
+            cp.start(("xr", p), npiece(x, p), npiece(x, p), xdev(1))
+        else:
+            cp.start(("xl", p), npiece(x, p), npiece(x, p), xdev(3))
+    for p in (2, 3):
         cp.start(("xr", p), npiece(x, p), npiece(x, p), xdev(1))
         cp.start(("xl", 3 - p), npiece(x, 3 - p), npiece(x, 3 - p), xdev(3))
     cp.arrive(("er", 0), wslot(c, z, y + 3, RA, WR - RA), ydev(1))
@@ -238,14 +267,14 @@
 
     def project(offsets, first):
         rows = len(offsets) * TB
-        acc[0:rows, :] = jnp.zeros((rows, 6 * DH), jnp.float32)
+        pacc[0:rows, :] = jnp.zeros((rows, 6 * DH), jnp.float32)
 
         @pl.loop(0, D // 512)
         def _(f):
             cols = pl.ds(pl.multiple_of(f * 512, 512), 512)
             lhs = jnp.concatenate([n_ref[(x + d) % 4, :, cols] for d in offsets], axis=0)
             rhs = jnp.concatenate([wbuf[yy, 0:DH, cols] for yy in range(4)] + [wbuf[yy, DH:WR, cols] for yy in range(4)], axis=0)
-            acc[0:rows, :] += nt(lhs, rhs)
+            pacc[0:rows, :] += nt(lhs, rhs)
 
         for n, d in enumerate(offsets):
             i = first + n
@@ -253,12 +282,12 @@
             r = pl.ds(n * TB, TB)
             cos, sin = rope_block(fine_ref, coarse_ref, 4 * xx + y)
             turn = lambda t: (t * cos + swap_pairs(t) * sin).astype(jnp.bfloat16)
-            a, b = acc[r, 4 * DH:5 * DH], acc[r, 5 * DH:6 * DH]
+            a, b = pacc[r, 4 * DH:5 * DH], pacc[r, 5 * DH:6 * DH]
             pick = lambda p0, p1, p2, p3: jnp.where(lane < 32, p0, jnp.where(lane < 64, p1, jnp.where(lane < 96, p2, p3)))
             key = turn(pick(a, pltpu.roll(a, 96, 1), pltpu.roll(b, 64, 1), pltpu.roll(b, 32, 1)))
             val = pick(pltpu.roll(a, 96, 1), pltpu.roll(a, 64, 1), pltpu.roll(b, 32, 1), b).astype(jnp.bfloat16)
             for dy in range(4):
-                q = turn(acc[r, pl.ds(pl.multiple_of((y + dy) % 4 * DH, DH), DH)])
+                q = turn(pacc[r, pl.ds(pl.multiple_of((y + dy) % 4 * DH, DH), DH)])
                 dst = qkv_ref.at[xx, y] if dy == 0 else stage.at[i, dy - 1]
                 dst[:, 0:DH] = q
                 dst[:, DH:2 * DH] = key
@@ -266,6 +295,8 @@
             for dy in (2, 1, 3):
                 cp.start(("q", i, dy), stage.at[i, dy - 1], qkv_ref.at[xx, y], ydev(dy))
 
+    loads["fine"].wait()
+    loads["coarse"].wait()
     project((0,), 0)
     for p in (2, 3):
         cp.arrive(("xr", p), npiece(x + 3, p), xdev(1))
@@ -278,41 +309,11 @@
     for i, d in enumerate((0, 3, 1, 2)):
         for dy in range(1, 4):
             cp.arrive(("q", i, dy), qkv_ref.at[(x + d) % 4, (y - dy) % 4], ydev(dy))
-    cp.drain()
-
-
-def front(h, gain, w, fine, coarse):
-    vmem = pl.BlockSpec(memory_space=pltpu.VMEM)
-    return pl.pallas_call(
-        front_kernel,
-        out_shape=(jax.ShapeDtypeStruct((4, TB, D), jnp.bfloat16), jax.ShapeDtypeStruct((4, 4, TB, 3 * DH), jnp.bfloat16)),
-        in_specs=[vmem] * 5,
-        out_specs=(vmem,) * 2,
-        scratch_shapes=[
-            pltpu.VMEM((4, WR, D), jnp.bfloat16),
-            pltpu.VMEM((3 * TB, 6 * DH), jnp.float32),
-            pltpu.VMEM((4, 3, TB, 3 * DH), jnp.bfloat16),
-            pltpu.SemaphoreType.DMA((FRONT_SEMS,)),
-            pltpu.SemaphoreType.DMA((FRONT_SEMS,)),
-        ],
-        compiler_params=pltpu.CompilerParams(vmem_limit_bytes=40 << 20, collective_id=0, has_side_effects=True),
-        name="front",
-    )(h, gain, w, fine, coarse)
-
-
-TAIL_SEMS = 8 + 32 + 7
-
-
-def tail_kernel(qkv_ref, g_ref, docs_row, docs_col, n_ref, fine_ref, coarse_ref, att_ref, gq_ref, gk_ref, gv_ref,
-                kt, vt, s_scr, p_scr, acc, dk_acc, dv_acc, d_scr, dsend, drecv,
-                rbuf, dt, own, cstage, cbuf, hstage, hbuf, fstage, fbuf, zstage, zbuf, ssem, rsem):
-    c, z, x, y = place()
-    ydev = lambda d: {"sp": x * 4 + (y + d) % 4}
-    zdev = lambda d: {"fsdp": (z + d) % 8}
-    other = {"bucket": 1 - c}
-    greet([ydev(1), ydev(2), ydev(3), other] + [zdev(d) for d in range(1, 8)])()
-    cp = Copies(ssem, rsem)
-    q_ref, k_ref, v_ref = (qkv_ref.at[:, pl.ds(part * DH, DH)] for part in range(3))
+
+
+    q_ref, k_ref, v_ref = (Part(qkv_ref.reshape(SEQ, 3 * DH), part) for part in range(3))
+    loads["g"].wait()
+    loads["docs"].wait()
 
     def exchange(i, dy):
         return pltpu.make_async_remote_copy(
@@ -412,7 +413,11 @@
             v = v_ref[krows, :]
             key = lax.broadcasted_iota(jnp.int32, (span, QB), 0) + first
             qry = lax.broadcasted_iota(jnp.int32, (span, QB), 1) + i * QB
-            same = docs_col[krows, :] == docs_row[i]
+            def docs(start, size):
+                rows = [docs_ref[:, pl.ds(pl.multiple_of(start + o, 128), 128)] for o in range(0, size, 128)]
+                return jnp.concatenate(rows, axis=1).astype(jnp.float32)
+
+            same = jnp.broadcast_to(docs(first, span), (128, span)).T[:, 0:1] == docs(i * QB, QB)
             s = jnp.where((key <= qry) & same, nt(k, q), NEG)
             m = jnp.max(s, axis=0, keepdims=True)
             p = jnp.exp2((s - m) * EXP_C)
@@ -496,21 +501,41 @@
     for t in range(7):
         cp.arrive(("z", t), zbuf.at[t], zdev(order[t]))
         total = total + zbuf[t].astype(jnp.float32)
-    gq_ref[...] = total[0:DH].T
-    gk_ref[...] = total[DH:DH + 32].T
-    gv_ref[...] = total[DH + 32:WR].T
+    grad_ref[...] = total
     cp.drain()
 
 
-def tail(qkv, g, docs, n, fine, coarse):
-    vmem = pl.BlockSpec(memory_space=pltpu.VMEM)
+def finish_kernel(att_ref, grad_ref, out_ref, gq_ref, gk_ref, gv_ref):
+    out_ref[...] = att_ref[...]
+    gq_ref[...] = grad_ref[0:DH].T
+    gk_ref[...] = grad_ref[DH:DH + 32].T
+    gv_ref[...] = grad_ref[DH + 32:WR].T
+
+
+def block(h, gain, wq, wk, wv, g, docs, fine, coarse):
+    vmem, hbm = pl.BlockSpec(memory_space=pltpu.VMEM), pl.BlockSpec(memory_space=pl.ANY)
     bf, f32, nb = jnp.bfloat16, jnp.float32, SEQ // KB
-    return pl.pallas_call(
-        tail_kernel,
-        out_shape=(jax.ShapeDtypeStruct((SEQ, DH), bf),) + tuple(jax.ShapeDtypeStruct((WF, w), f32) for w in (DH, 32, 32)),
-        in_specs=[vmem] * 7,
-        out_specs=(vmem,) * 4,
+    att, grad = pl.pallas_call(
+        block_kernel,
+        out_shape=(jax.ShapeDtypeStruct((SEQ, DH), bf), jax.ShapeDtypeStruct((WR, WF), f32)),
+        in_specs=[hbm] * 9,
+        out_specs=(vmem,) * 2,
         scratch_shapes=[
+            pltpu.VMEM((TB, D), bf),
+            pltpu.VMEM((1, D), f32),
+            pltpu.VMEM((WF, DH), bf),
+            pltpu.VMEM((WF, 32), bf),
+            pltpu.VMEM((WF, 32), bf),
+            pltpu.VMEM((SEQ, DH), bf),
+            pltpu.VMEM((1, SEQ), jnp.int32),
+            pltpu.VMEM((2, TB, DH), f32),
+            pltpu.VMEM((2, 16, DH), f32),
+            pltpu.VMEM((WR, WF), bf),
+            pltpu.VMEM((4, TB, D), bf),
+            pltpu.VMEM((4, 4, TB, 3 * DH), bf),
+            pltpu.VMEM((4, WR, D), bf),
+            pltpu.VMEM((2 * TB, 6 * DH), f32),
+            pltpu.VMEM((4, 3, TB, 3 * DH), bf),
             pltpu.VMEM((nb, DH, KB), bf),
             pltpu.VMEM((nb, DH, KB), bf),
             pltpu.VMEM((nb, KB, QB), f32),
@@ -532,20 +557,26 @@
             pltpu.VMEM((8, 2, WR, WF), bf),
             pltpu.VMEM((7, WR, WF), bf),
             pltpu.VMEM((7, WR, WF), bf),
-            pltpu.SemaphoreType.DMA((TAIL_SEMS,)),
-            pltpu.SemaphoreType.DMA((TAIL_SEMS,)),
+            pltpu.SemaphoreType.DMA((SEMS,)),
+            pltpu.SemaphoreType.DMA((SEMS,)),
+            pltpu.SemaphoreType.DMA((9,)),
         ],
-        compiler_params=pltpu.CompilerParams(vmem_limit_bytes=56 << 20, collective_id=1, has_side_effects=True),
-        name="tail",
-    )(qkv, g, docs.reshape(SEQ // QB, 1, QB), docs.reshape(SEQ, 1), n, fine, coarse)
+        compiler_params=pltpu.CompilerParams(vmem_limit_bytes=62 << 20, collective_id=0, has_side_effects=True),
+        name="block",
+    )(h, gain, wq, wk, wv, g, docs, fine, coarse)
+    return pl.pallas_call(
+        finish_kernel,
+        out_shape=(jax.ShapeDtypeStruct((SEQ, DH), bf),) + tuple(jax.ShapeDtypeStruct((WF, w), f32) for w in (DH, 32, 32)),
+        in_specs=[vmem] * 2,
+        out_specs=(vmem,) * 4,
+        name="finish",
+    )(att, grad)
 
 
 def local(hidden_states, norm_gain, w_query, w_key, w_value, out_grad, short_docs):
     fine, coarse = (jnp.asarray(t) for t in rope_tables())
-    w = jnp.concatenate([w_query.T, w_key.T, w_value.T], axis=0)
-    n, qkv = front(hidden_states.reshape(TB, D), norm_gain.reshape(1, D), w, fine, coarse)
-    docs = jnp.where(lax.axis_index("bucket") == 0, 0, short_docs[0])
-    att, gq, gk, gv = tail(qkv.reshape(SEQ, 3 * DH), out_grad.reshape(SEQ, DH), docs, n, fine, coarse)
+    att, gq, gk, gv = block(hidden_states.reshape(TB, D), norm_gain.reshape(1, D), w_query, w_key, w_value,
+                            out_grad.reshape(SEQ, DH), short_docs, fine, coarse)
     return att.reshape(1, 1, SEQ, DH), gq, gk, gv
 
 

time: 144 us -> 127 us (0.88)
  local copies, waits for them, and re-layouts: 15.6 us -> 4.51 us
  Pallas kernels: 125 us -> 121 us
    unnamed x17 -> x8, local copies, waits for them, and re-layouts: 14.2 us -> 4.51 us
    pallas_call x2, Pallas kernels: 125 us -> 121 us  [the longest x1 119 us: block(): pl.pallas_call(block_kernel, out_shape=(jax.ShapeDtypeStruct((SEQ, DH), b...]
where the time goes in v3:
time: 127 us; the launch traced here: 126 us
  Pallas kernels  121 us (95%)
  local copies, waits for them, and re-layouts  4.51 us (4%)
    pallas_call x1, Pallas kernels, block(): pl.pallas_call(block_kernel, out_shape=(jax.ShapeDtypeStruct((SEQ, DH), b...  119 us
    unnamed x8, local copies, waits for them, and re-layouts  4.51 us

profile of v3, /device:TPU:2, one launch (start us, length us, event | category | flops | bytes accessed | tf_op | source)
XLA Modules:
  0.0 126.3 jit_solution(1931399010053167271)
XLA Ops:
  0.6 0.0 copy-start.1
  0.6 1.5 %copy.13.wk_hbm = bf16[256,32]{1,0:T(8,128)(2,1)} copy(bf16[256,32]{0,1:T(8,128)(2,1)} %param.12) | data formatting | bytes 32768 | tf_op args[3]
  2.1 0.0 copy-done.1
  2.1 0.7 copy.14.wv_hbm
  2.8 119.0 %block.1 = (bf16[2048,128]{1,0:T(8,128)(2,1)}, f32[192,256]{1,0:T(8,128)}) custom-call(bf16[128,4096]{1,0:T(8,128)(2,1)} %bitcast.4, f32[1,4096]{1,0:T(1,128)} %bitcast.6, bf16[256,128]{1,0:T(8,128)(2,1)} %wq_hbm.1, bf16[256,32]{1,0:T(8,128)(2,1)} %copy.13.wk_hbm, bf16[256,32]{1,0:T(8,128)(2,1)} %copy.14.wv_hbm, bf16[2048,128]{1,0:T(8,128)(2,1)} %bitcast.5, ...), custom_call_target="tpu_custom_call" | custom-call | tf_op jit(solution)/shard_map/block/pallas_call | solution.py:518
  121.9 2.1 %finish.1 = (bf16[2048,128]{1,0:T(8,128)(2,1)}, f32[256,128]{1,0:T(8,128)}, f32[256,32]{1,0:T(8,128)}, f32[256,32]{1,0:T(8,128)}) custom-call(bf16[2048,128]{1,0:T(8,128)(2,1)} %get-tuple-element.10.att_ref, f32[192,256]{1,0:T(8,128)} %get-tuple-element.11.grad_ref), custom_call_target="tpu_custom_call" | custom-call | tf_op jit(solution)/shard_map/finish/pallas_call | solution.py:567
  124.0 0.0 copy-start
  124.0 1.6 %copy.15 = f32[256,32]{0,1:T(8,128)} copy(f32[256,32]{1,0:T(8,128)} %get-tuple-element.18) | data formatting | bytes 65536
  125.6 0.0 copy-done
  125.6 0.7 copy.16
Async XLA Ops:
  0.6 1.5 %copy-start.1 = (bf16[256,32]{0,1:T(8,128)(2,1)S(1)}, bf16[256,32]{0,1:T(8,128)(2,1)}, u32[]{:S(2)}) copy-start(bf16[256,32]{0,1:T(8,128)(2,1)} %param.13) | copy-start | bytes 49156
  124.0 1.6 %copy-start = (f32[256,32]{1,0:T(8,128)S(1)}, f32[256,32]{1,0:T(8,128)}, u32[]{:S(2)}) copy-start(f32[256,32]{1,0:T(8,128)} %get-tuple-element.19) | copy-start | bytes 98308

commit v4 on v3

--- a/solution.py
+++ b/solution.py
@@ -56,6 +56,7 @@
 WF = 256
 EPS = 1e-5
 RA, HA, HB = 112, 48, 32
+R1, H1 = 144, 64
 
 
 class Copies:
@@ -92,7 +93,7 @@
     return lambda: pl.semaphore_wait(barrier, len(devs))
 
 
-SEMS = 7 + 32 + 4 + 28 + 16 + 12 + 12 + 8 + 32 + 7
+SEMS = 7 + 32 + 4 + 28 + 16 + 12 + 12 + 8 + 32 + 7 + 10
 
 
 class Part:
@@ -107,10 +108,10 @@
                  h_ref, gain_ref, wq_ref, wk_ref, wv_ref, g_ref, docs_ref, fine_ref, coarse_ref, w_ref,
                  n_ref, qkv4_ref, wbuf, pacc, stage,
                  kt, vt, s_scr, p_scr, acc, dk_acc, dv_acc, d_scr, dsend, drecv,
-                 rbuf, dt, own, cstage, cbuf, hstage, hbuf, fstage, fbuf, zstage, zbuf, ssem, rsem, lsem):
+                 rbuf, dt, own, cstage, cbuf, hstage, hbuf, fstage, fbuf, zstage, zbuf, rstage2, rbuf2, ystage, ybuf, ssem, rsem, lsem):
     loads = {}
-    for name, src, dst in (("wq", wq_hbm, wq_ref), ("wk", wk_hbm, wk_ref), ("wv", wv_hbm, wv_ref), ("h", h_hbm, h_ref),
-                           ("gain", gain_hbm, gain_ref), ("fine", fine_hbm, fine_ref), ("coarse", coarse_hbm, coarse_ref),
+    for name, src, dst in (("h", h_hbm, h_ref), ("gain", gain_hbm, gain_ref), ("wq", wq_hbm, wq_ref), ("wk", wk_hbm, wk_ref),
+                           ("wv", wv_hbm, wv_ref), ("fine", fine_hbm, fine_ref), ("coarse", coarse_hbm, coarse_ref),
                            ("g", g_hbm, g_ref), ("docs", docs_hbm, docs_ref)):
         loads[name] = pltpu.make_async_copy(src, dst, lsem.at[len(loads)])
         loads[name].start()
@@ -129,11 +130,16 @@
     for name in ("wq", "wk", "wv"):
         loads[name].wait()
     w_ref[0:DH] = wq_ref[...].T
-    w_ref[DH:DH + 32] = wk_ref[...].T
-    w_ref[DH + 32:WR] = wv_ref[...].T
+    w_ref[DH:DH + 32] = wk_ref[...]
+    w_ref[DH + 32:WR] = wv_ref[...]
     wslot(c, z, y)[...] = w_ref[...]
+    loads["h"].wait()
+    loads["gain"].wait()
+    for r in range(0, TB, 32):
+        rows = h_ref[r:r + 32, :].astype(jnp.float32)
+        inv = lax.rsqrt(jnp.mean(rows * rows, axis=1, keepdims=True) + EPS)
+        n_ref[x, r:r + 32, :] = (rows * inv * gain_ref[...]).astype(jnp.bfloat16)
     wait_all()
-    loads["gain"].wait()
     cp = Copies(ssem, rsem)
     zoff = [0, -1, -2, -3, -4, 1, 2, 3]
     yoff = [0, 3, 1, 2]
@@ -179,6 +185,9 @@
     def npiece(xx, p):
         return n_ref.at[xx % 4, pl.ds(p * 32, 32), :]
 
+    for p in range(4):
+        cp.start(("xr", p), npiece(x, p), npiece(x, p), xdev(1))
+        cp.start(("xl", 3 - p), npiece(x, 3 - p), npiece(x, 3 - p), xdev(3))
     own_a, own_b = w_ref.at[pl.ds(0, RA), :], w_ref.at[pl.ds(RA, WR - RA), :]
     cp.start(("zr", 1), own_a, wslot(c, z, y, 0, RA), zdev(1))
     cp.start(("zl", 1), own_a, wslot(c, z, y, 0, RA), zdev(7))
@@ -187,18 +196,6 @@
     spread(0)
     chain(0, 0, True)
     chain(0, 0, False)
-    loads["h"].wait()
-    for p in (0, 3, 1, 2):
-        rows = h_ref[p * 32:(p + 1) * 32, :].astype(jnp.float32)
-        inv = lax.rsqrt(jnp.mean(rows * rows, axis=1, keepdims=True) + EPS)
-        n_ref[x, p * 32:(p + 1) * 32, :] = (rows * inv * gain_ref[...]).astype(jnp.bfloat16)
-        if p in (0, 1):
-            cp.start(("xr", p), npiece(x, p), npiece(x, p), xdev(1))
-        else:
-            cp.start(("xl", p), npiece(x, p), npiece(x, p), xdev(3))
-    for p in (2, 3):
-        cp.start(("xr", p), npiece(x, p), npiece(x, p), xdev(1))
-        cp.start(("xl", 3 - p), npiece(x, 3 - p), npiece(x, 3 - p), xdev(3))
     cp.arrive(("er", 0), wslot(c, z, y + 3, RA, WR - RA), ydev(1))
     part = wslot(c, z, y + 3, RA, HB)
     cp.start(("ea", 0), part, part, ydev(1))
@@ -451,8 +448,7 @@
             dt[yy, DH:DH + 32, cols] = key[yy * 32:(yy + 1) * 32]
             dt[yy, DH + 32:WR, cols] = val[yy * 32:(yy + 1) * 32]
 
-    order = (4, 3, 5, 2, 6, 1, 7, 0)
-    half = WR // 2
+    order = (4, 5, 3, 6, 2, 7, 1, 0)
 
     def product(core, dz):
         col = pl.multiple_of((core * 8 + (z + dz) % 8) * WF, WF)
@@ -467,49 +463,73 @@
     def meet(t):
         cp.arrive(("c", t), cbuf.at[t], other)
         own[t] += cbuf[t].astype(jnp.float32)
-        hstage[t, 0] = own[t, (y + 2) % 4, 0:half].astype(jnp.bfloat16)
-        hstage[t, 1] = own[t, (y + 2) % 4, half:WR].astype(jnp.bfloat16)
-        cp.start(("a", t), hstage.at[t, 0], hbuf.at[t, 0], ydev(1))
+        hstage[t, 0, 0:H1] = own[t, (y + 2) % 4, 0:H1].astype(jnp.bfloat16)
+        hstage[t, 1] = own[t, (y + 2) % 4, H1:R1].astype(jnp.bfloat16)
+        cp.start(("a", t), hstage.at[t, 0, pl.ds(0, H1)], hbuf.at[t, 0, pl.ds(0, H1)], ydev(1))
         cp.start(("b", t), hstage.at[t, 1], hbuf.at[t, 1], ydev(3))
+        if order[t] in (4, 5):
+            ring(t, "n", own[t, :, R1:WR], rstage2, rbuf2)
+
+    def ring(t, kind, value, sent, got):
+        dz = order[t]
+        right = dz <= 4
+        step = 4 - dz if right else dz - 5
+        name, peer, first = (kind + "r", zdev(1), 0) if right else (kind + "l", zdev(7), 4)
+        if step > 0:
+            cp.arrive((name, step - 1), got.at[first + step - 1], peer)
+            value = value + got[first + step - 1].astype(jnp.float32)
+        sent[first + step] = value.astype(jnp.bfloat16)
+        cp.start((name, step), sent.at[first + step], got.at[first + step], peer)
+
+    def ring_end(kind, got):
+        cp.arrive((kind + "r", 3), got.at[3], zdev(1))
+        cp.arrive((kind + "l", 2), got.at[6], zdev(7))
+        return got[3].astype(jnp.float32) + got[6].astype(jnp.float32)
 
     def pass_on(t):
-        cp.arrive(("a", t), hbuf.at[t, 0], ydev(1))
-        fstage[t, 0, 0:half] = (own[t, (y + 1) % 4, 0:half] + hbuf[t, 0].astype(jnp.float32)).astype(jnp.bfloat16)
-        fstage[t, 0, half:WR] = own[t, (y + 1) % 4, half:WR].astype(jnp.bfloat16)
+        cp.arrive(("a", t), hbuf.at[t, 0, pl.ds(0, H1)], ydev(1))
+        fstage[t, 0, 0:H1] = (own[t, (y + 1) % 4, 0:H1] + hbuf[t, 0, 0:H1].astype(jnp.float32)).astype(jnp.bfloat16)
+        fstage[t, 0, H1:R1] = own[t, (y + 1) % 4, H1:R1].astype(jnp.bfloat16)
         cp.start(("r", t), fstage.at[t, 0], fbuf.at[t, 0], ydev(1))
         cp.arrive(("b", t), hbuf.at[t, 1], ydev(3))
-        fstage[t, 1, 0:half] = own[t, (y + 3) % 4, 0:half].astype(jnp.bfloat16)
-        fstage[t, 1, half:WR] = (own[t, (y + 3) % 4, half:WR] + hbuf[t, 1].astype(jnp.float32)).astype(jnp.bfloat16)
+        fstage[t, 1, 0:H1] = own[t, (y + 3) % 4, 0:H1].astype(jnp.bfloat16)
+        fstage[t, 1, H1:R1] = (own[t, (y + 3) % 4, H1:R1] + hbuf[t, 1].astype(jnp.float32)).astype(jnp.bfloat16)
         cp.start(("l", t), fstage.at[t, 1], fbuf.at[t, 1], ydev(3))
+        if order[t] not in (0, 4, 5):
+            ring(t, "n", own[t, :, R1:WR], rstage2, rbuf2)
 
     def home(t):
         cp.arrive(("r", t), fbuf.at[t, 0], ydev(1))
         cp.arrive(("l", t), fbuf.at[t, 1], ydev(3))
-        total = own[t, y] + fbuf[t, 0].astype(jnp.float32) + fbuf[t, 1].astype(jnp.float32)
+        total = own[t, y, 0:R1] + fbuf[t, 0].astype(jnp.float32) + fbuf[t, 1].astype(jnp.float32)
         if order[t] == 0:
-            own[t, 0] = total
+            grad_ref[0:R1] = total
         else:
-            zstage[t] = total.astype(jnp.bfloat16)
-            cp.start(("z", t), zstage.at[t], zbuf.at[t], zdev(order[t]))
-
-    for t in range(8 + 3):
-        for delay, stage in ((0, compute), (1, meet), (2, pass_on), (3, home)):
+            ring(t, "m", total, zstage, zbuf)
+
+    for t in range(8 + 6):
+        for delay, part in ((0, compute), (2, meet), (4, pass_on), (6, home)):
             if 0 <= t - delay < 8:
-                stage(t - delay)
-
-    total = own[7, 0]
-    for t in range(7):
-        cp.arrive(("z", t), zbuf.at[t], zdev(order[t]))
-        total = total + zbuf[t].astype(jnp.float32)
-    grad_ref[...] = total
+                part(t - delay)
+
+    own[7, :, R1:WR] += ring_end("n", rbuf2)
+    for dy in (2, 1, 3):
+        ystage[dy - 1] = own[7, (y + dy) % 4, R1:WR].astype(jnp.bfloat16)
+        cp.start(("v", dy), ystage.at[dy - 1], ybuf.at[dy - 1], ydev(dy))
+    grad_ref[0:R1] += ring_end("m", zbuf)
+    total = own[7, y, R1:WR]
+    for dy in (1, 3, 2):
+        cp.arrive(("v", dy), ybuf.at[dy - 1], ydev(dy))
+        total = total + ybuf[dy - 1].astype(jnp.float32)
+    grad_ref[R1:WR] = total
     cp.drain()
 
 
 def finish_kernel(att_ref, grad_ref, out_ref, gq_ref, gk_ref, gv_ref):
     out_ref[...] = att_ref[...]
     gq_ref[...] = grad_ref[0:DH].T
-    gk_ref[...] = grad_ref[DH:DH + 32].T
-    gv_ref[...] = grad_ref[DH + 32:WR].T
+    gk_ref[...] = grad_ref[DH:DH + 32]
+    gv_ref[...] = grad_ref[DH + 32:WR]
 
 
 def block(h, gain, wq, wk, wv, g, docs, fine, coarse):
@@ -524,8 +544,8 @@
             pltpu.VMEM((TB, D), bf),
             pltpu.VMEM((1, D), f32),
             pltpu.VMEM((WF, DH), bf),
-            pltpu.VMEM((WF, 32), bf),
-            pltpu.VMEM((WF, 32), bf),
+            pltpu.VMEM((32, WF), bf),
+            pltpu.VMEM((32, WF), bf),
             pltpu.VMEM((SEQ, DH), bf),
             pltpu.VMEM((1, SEQ), jnp.int32),
             pltpu.VMEM((2, TB, DH), f32),
@@ -551,12 +571,16 @@
             pltpu.VMEM((8, 4, WR, WF), f32),
             pltpu.VMEM((8, 4, WR, WF), bf),
             pltpu.VMEM((8, 4, WR, WF), bf),
-            pltpu.VMEM((8, 2, WR // 2, WF), bf),
-            pltpu.VMEM((8, 2, WR // 2, WF), bf),
-            pltpu.VMEM((8, 2, WR, WF), bf),
-            pltpu.VMEM((8, 2, WR, WF), bf),
-            pltpu.VMEM((7, WR, WF), bf),
-            pltpu.VMEM((7, WR, WF), bf),
+            pltpu.VMEM((8, 2, R1 - H1, WF), bf),
+            pltpu.VMEM((8, 2, R1 - H1, WF), bf),
+            pltpu.VMEM((8, 2, R1, WF), bf),
+            pltpu.VMEM((8, 2, R1, WF), bf),
+            pltpu.VMEM((7, R1, WF), bf),
+            pltpu.VMEM((7, R1, WF), bf),
+            pltpu.VMEM((7, 4, WR - R1, WF), bf),
+            pltpu.VMEM((7, 4, WR - R1, WF), bf),
+            pltpu.VMEM((3, WR - R1, WF), bf),
+            pltpu.VMEM((3, WR - R1, WF), bf),
             pltpu.SemaphoreType.DMA((SEMS,)),
             pltpu.SemaphoreType.DMA((SEMS,)),
             pltpu.SemaphoreType.DMA((9,)),
@@ -566,7 +590,7 @@
     )(h, gain, wq, wk, wv, g, docs, fine, coarse)
     return pl.pallas_call(
         finish_kernel,
-        out_shape=(jax.ShapeDtypeStruct((SEQ, DH), bf),) + tuple(jax.ShapeDtypeStruct((WF, w), f32) for w in (DH, 32, 32)),
+        out_shape=(jax.ShapeDtypeStruct((SEQ, DH), bf),) + tuple(jax.ShapeDtypeStruct(s, f32) for s in ((WF, DH), (32, WF), (32, WF))),
         in_specs=[vmem] * 2,
         out_specs=(vmem,) * 4,
         name="finish",
@@ -575,9 +599,9 @@
 
 def local(hidden_states, norm_gain, w_query, w_key, w_value, out_grad, short_docs):
     fine, coarse = (jnp.asarray(t) for t in rope_tables())
-    att, gq, gk, gv = block(hidden_states.reshape(TB, D), norm_gain.reshape(1, D), w_query, w_key, w_value,
+    att, gq, gk, gv = block(hidden_states.reshape(TB, D), norm_gain.reshape(1, D), w_query, w_key.T, w_value.T,
                             out_grad.reshape(SEQ, DH), short_docs, fine, coarse)
-    return att.reshape(1, 1, SEQ, DH), gq, gk, gv
+    return att.reshape(1, 1, SEQ, DH), gq, gk.T, gv.T
 
 
 def solution(mesh):

time: 127 us -> 116 us (0.913)
  Pallas kernels: 121 us -> 115 us
  local copies, waits for them, and re-layouts: 4.51 us -> 0 us
    pallas_call x1, Pallas kernels: 119 us -> 113 us  [block(): pl.pallas_call(block_kernel, out_shape=(jax.ShapeDtypeStruct((SEQ, DH), b...]
    unnamed x8 -> x0, local copies, waits for them, and re-layouts: 4.51 us -> none
where the time goes in v4:
time: 116 us
  Pallas kernels  115 us (99%)
    pallas_call x1, Pallas kernels, block(): pl.pallas_call(block_kernel, out_shape=(jax.ShapeDtypeStruct((SEQ, DH), b...  113 us

profile of v4, /device:TPU:2, one launch (start us, length us, event | category | flops | bytes accessed | tf_op | source)
XLA Modules:
  0.0 115.6 jit_solution(14733810787758724378)
XLA Ops:
  0.6 113.0 %block.1 = (bf16[2048,128]{1,0:T(8,128)(2,1)}, f32[192,256]{1,0:T(8,128)}) custom-call(bf16[128,4096]{1,0:T(8,128)(2,1)} %bitcast.8, f32[1,4096]{1,0:T(1,128)} %bitcast.10, bf16[256,128]{1,0:T(8,128)(2,1)} %wq_hbm.1, bf16[32,256]{1,0:T(8,128)(2,1)} %bitcast.11, bf16[32,256]{1,0:T(8,128)(2,1)} %bitcast.12, bf16[2048,128]{1,0:T(8,128)(2,1)} %bitcast.9, ...), custom_call_target="tpu_custom_call" | custom-call | tf_op jit(solution)/shard_map/block/pallas_call | solution.py:538
  113.6 2.0 %finish.1 = (bf16[2048,128]{1,0:T(8,128)(2,1)}, f32[256,128]{1,0:T(8,128)}, f32[32,256]{1,0:T(8,128)}, f32[32,256]{1,0:T(8,128)}) custom-call(bf16[2048,128]{1,0:T(8,128)(2,1)} %get-tuple-element.10.att_ref, f32[192,256]{1,0:T(8,128)} %get-tuple-element.11.grad_ref), custom_call_target="tpu_custom_call" | custom-call | tf_op jit(solution)/shard_map/finish/pallas_call | solution.py:591

commit v5 on v4

--- a/solution.py
+++ b/solution.py
@@ -217,45 +217,52 @@
         zz = z + zoff[zi]
         cp.start(("cb", zi), wall(c, zz, RA, WR - RA), wall(c, zz, RA, WR - RA), other)
 
-    done, waiting = [0], []
-    for step in range(1, 5):
+    def a_step(step):
         src = wslot(c, z - step, y, 0, RA)
         cp.arrive(("zr", step), src, zdev(1))
         if step < 4:
             cp.start(("zr", step + 1), src, src, zdev(1))
         spread(step)
-        fresh = [step]
         if step < 4:
             src = wslot(c, z + step, y, 0, RA)
             cp.arrive(("zl", step), src, zdev(7))
             if step < 3:
                 cp.start(("zl", step + 1), src, src, zdev(7))
             spread(4 + step)
-            fresh.append(4 + step)
-        if step == 1:
-            cp.arrive(("ea", 0), wslot(c, z, y + 2, RA, HB), ydev(1))
-            cp.arrive(("eb", 0), wslot(c, z, y + 2, RA + HB, WR - RA - HB), ydev(3))
-            chain(3, 0, True)
-            chain(3, 0, False)
-            core_b(0)
-        for zi in done:
-            serve(zi)
+
+    def b_step(step):
         for yk in range(4):
             chain(yk, step, True)
             chain(yk, step, False)
         core_b(step)
         if step < 4:
             core_b(4 + step)
-        for zi in waiting:
-            last(zi)
-        waiting, done = done, fresh
-        if step == 3:
-            relay_x(0)
-            relay_x(1)
-    for zi in done:
-        serve(zi)
-    for zi in waiting + done:
-        last(zi)
+
+    def each(act, *zis):
+        for zi in zis:
+            act(zi)
+
+    a_step(1)
+    cp.arrive(("ea", 0), wslot(c, z, y + 2, RA, HB), ydev(1))
+    cp.arrive(("eb", 0), wslot(c, z, y + 2, RA + HB, WR - RA - HB), ydev(3))
+    chain(3, 0, True)
+    chain(3, 0, False)
+    core_b(0)
+    a_step(2)
+    each(serve, 0)
+    b_step(1)
+    a_step(3)
+    each(serve, 1, 5)
+    each(last, 0)
+    a_step(4)
+    each(serve, 2, 6)
+    b_step(2)
+    each(relay_x, 0, 1)
+    each(serve, 3, 7, 4)
+    each(last, 1, 5, 2, 6)
+    b_step(3)
+    each(last, 3, 7, 4)
+    b_step(4)
     for zi in range(8):
         cp.arrive(("ca", zi), wall(1 - c, z + zoff[zi], 0, RA), other)
         cp.arrive(("cb", zi), wall(1 - c, z + zoff[zi], RA, WR - RA), other)

time: 116 us -> 115 us (level)
    pallas_call x1, Pallas kernels: 113 us -> 112 us  [block(): pl.pallas_call(block_kernel, out_shape=(jax.ShapeDtypeStruct((SEQ, DH), b...]
where the time goes in v5:
time: 115 us; the launch traced here: 114 us
  Pallas kernels  114 us (99%)
    pallas_call x1, Pallas kernels, block(): pl.pallas_call(block_kernel, out_shape=(jax.ShapeDtypeStruct((SEQ, DH), b...  112 us

profile of v5, /device:TPU:2, one launch (start us, length us, event | category | flops | bytes accessed | tf_op | source)
XLA Modules:
  0.0 114.4 jit_solution(9335008102758200091)
XLA Ops:
  0.6 111.8 %block.1 = (bf16[2048,128]{1,0:T(8,128)(2,1)}, f32[192,256]{1,0:T(8,128)}) custom-call(bf16[128,4096]{1,0:T(8,128)(2,1)} %bitcast.8, f32[1,4096]{1,0:T(1,128)} %bitcast.10, bf16[256,128]{1,0:T(8,128)(2,1)} %wq_hbm.1, bf16[32,256]{1,0:T(8,128)(2,1)} %bitcast.11, bf16[32,256]{1,0:T(8,128)(2,1)} %bitcast.12, bf16[2048,128]{1,0:T(8,128)(2,1)} %bitcast.9, ...), custom_call_target="tpu_custom_call" | custom-call | tf_op jit(solution)/shard_map/block/pallas_call | solution.py:545
  112.4 2.0 %finish.1 = (bf16[2048,128]{1,0:T(8,128)(2,1)}, f32[256,128]{1,0:T(8,128)}, f32[32,256]{1,0:T(8,128)}, f32[32,256]{1,0:T(8,128)}) custom-call(bf16[2048,128]{1,0:T(8,128)(2,1)} %get-tuple-element.10.att_ref, f32[192,256]{1,0:T(8,128)} %get-tuple-element.11.grad_ref), custom_call_target="tpu_custom_call" | custom-call | tf_op jit(solution)/shard_map/finish/pallas_call | solution.py:598

commit v6 on v5

--- a/solution.py
+++ b/solution.py
@@ -56,7 +56,7 @@
 WF = 256
 EPS = 1e-5
 RA, HA, HB = 112, 48, 32
-R1, H1 = 144, 64
+R1, H1 = 128, 64
 
 
 class Copies:

time: 115 us -> 113 us (0.983)
  Pallas kernels: 114 us -> 112 us
    pallas_call x1, Pallas kernels: 112 us -> 110 us  [block(): pl.pallas_call(block_kernel, out_shape=(jax.ShapeDtypeStruct((SEQ, DH), b...]
where the time goes in v6:
time: 113 us
  Pallas kernels  112 us (99%)
    pallas_call x1, Pallas kernels, block(): pl.pallas_call(block_kernel, out_shape=(jax.ShapeDtypeStruct((SEQ, DH), b...  110 us

profile of v6, /device:TPU:2, one launch (start us, length us, event | category | flops | bytes accessed | tf_op | source)
XLA Modules:
  0.0 113.0 jit_solution(5532668931884160170)
XLA Ops:
  0.6 110.4 %block.1 = (bf16[2048,128]{1,0:T(8,128)(2,1)}, f32[192,256]{1,0:T(8,128)}) custom-call(bf16[128,4096]{1,0:T(8,128)(2,1)} %bitcast.8, f32[1,4096]{1,0:T(1,128)} %bitcast.10, bf16[256,128]{1,0:T(8,128)(2,1)} %wq_hbm.1, bf16[32,256]{1,0:T(8,128)(2,1)} %bitcast.11, bf16[32,256]{1,0:T(8,128)(2,1)} %bitcast.12, bf16[2048,128]{1,0:T(8,128)(2,1)} %bitcast.9, ...), custom_call_target="tpu_custom_call" | custom-call | tf_op jit(solution)/shard_map/block/pallas_call | solution.py:545
  111.0 2.0 %finish.1 = (bf16[2048,128]{1,0:T(8,128)(2,1)}, f32[256,128]{1,0:T(8,128)}, f32[32,256]{1,0:T(8,128)}, f32[32,256]{1,0:T(8,128)}) custom-call(bf16[2048,128]{1,0:T(8,128)(2,1)} %get-tuple-element.10.att_ref, f32[192,256]{1,0:T(8,128)} %get-tuple-element.11.grad_ref), custom_call_target="tpu_custom_call" | custom-call | tf_op jit(solution)/shard_map/finish/pallas_call | solution.py:598
